TPU v7x, 32 devices: a whole 2x2x4 slice. The times are simulated.
32 devices in a mesh: groups: 2 (over y), seq: 4 (over z), head: 2 (over x), fsdp: 2 (over core).
Axes of the slice: x: 2, y: 2, z: 4, core: 2. Of those that a mesh axis runs over, the one named last changes fastest.
Arguments:
- residual_in: bfloat16 [16384, 2048], P(('groups', 'seq', 'fsdp'), 'head'), parts along dimension 0, may hold values from -6 to 6
- query_rows: bfloat16 [16384, 2048], P(('groups', 'seq', 'fsdp'), 'head'), parts along dimension 0, may hold values from -7 to 7
- key_rows: bfloat16 [16384, 2048], P(('groups', 'seq', 'fsdp'), 'head'), parts along dimension 0, may hold values from -7 to 7
- value_rows: bfloat16 [16384, 2048], P(('groups', 'seq', 'fsdp'), 'head'), parts along dimension 0, may hold values from -6 to 6
- bc_weight: bfloat16 [2048, 256], P(('head', 'fsdp')), may hold values from -0.125 to 0.125
- decay_rate: float32 [16384, 32], P(('groups', 'seq', 'fsdp'), 'head'), parts along dimension 0, may hold values from 0 to 0.8
- level_codes: int32 [16384, 18], P(('groups', 'seq', 'fsdp')), parts along dimension 0, may hold values from 0 to 255
- level_scale: float32 [18], replicated, may hold values from 0.05 to 1
- positions: int32 [16384], P(('groups', 'seq', 'fsdp')), parts along dimension 0, may hold values from 0 to 2047, as said below
- ssm_gain: float32 [2048], P('head'), may hold values from 0.25 to 1.75
Outputs:
- mixed_out: bfloat16 [16384, 2048], P(('groups', 'seq', 'fsdp'), 'head'), parts along dimension 0
There are 2 independent parts, one for each index of `groups`. A program takes and returns all parts, laid end to end along the dimension named above; an argument that names none is the same for every part. Nothing has to cross between parts.
Inputs may be any that keep to these rules, and one draw needn't show every extreme that they name: positions[t] is 0 where a document begins (always at t = 0) and positions[t - 1] + 1 elsewhere.
All inputs are finite; a program needn't handle non-finite values.
Results may differ from a plain program's by a relative error of at most 0.008.
Values may be sent and summed in bfloat16 or wider, within the bound.
A program may use at most 64 MiB of HBM per device.

v0:
```python
import math

import jax
import jax.numpy as jnp
from jax import lax
from jax.sharding import PartitionSpec as P

HEAD_DIM = 128
HEAD_VALUES = 64
STATES = 128
WINDOW = 128


def from_behind(x, axis, by):
    length = lax.axis_size(axis)
    pairs = [(i, i + by) for i in range(length) if 0 <= i + by < length]
    return lax.ppermute(x, axis, pairs)


def partner(x, axis, distance):
    return lax.ppermute(x, axis, [(i, i ^ 1 << distance) for i in range(lax.axis_size(axis))])


def widen(vector, repeat_count):
    return jnp.repeat(vector, repeat_count, axis=-1)


def window_attention(query_rows, key_rows, value_rows, edge_keys, edge_values, positions):
    row_count, local_width = query_rows.shape
    head_count = local_width // HEAD_DIM
    block_total = row_count // WINDOW
    key_blocks = jnp.concatenate([edge_keys, key_rows], axis=0).reshape(
        block_total + 1, WINDOW, head_count, HEAD_DIM
    )
    value_blocks = jnp.concatenate([edge_values, value_rows], axis=0).reshape(
        block_total + 1, WINDOW, head_count, HEAD_DIM
    )
    key_pairs = jnp.concatenate([key_blocks[:block_total], key_blocks[1:]], axis=1)
    value_pairs = jnp.concatenate([value_blocks[:block_total], value_blocks[1:]], axis=1)
    query_blocks = query_rows.reshape(block_total, WINDOW, head_count, HEAD_DIM)
    scores = jnp.einsum(
        "bqhd,bkhd->bhqk", query_blocks, key_pairs, preferred_element_type=jnp.float32
    ) / math.sqrt(HEAD_DIM)
    query_idx = jnp.arange(WINDOW, dtype=jnp.int32)[:, None]
    key_idx = jnp.arange(2 * WINDOW, dtype=jnp.int32)[None, :]
    distance = query_idx + WINDOW - key_idx
    doc_pos = positions.reshape(block_total, 1, WINDOW, 1)
    visible = (
        (distance >= 0)[None, None]
        & (distance < WINDOW)[None, None]
        & (distance[None, None] <= doc_pos)
    )
    masked = jnp.where(visible, scores, -jnp.inf)
    top_score = jnp.max(masked, axis=3, keepdims=True)
    weights = jnp.exp(masked - top_score)
    probabilities = (weights / jnp.sum(weights, axis=3, keepdims=True)).astype(jnp.bfloat16)
    attended = jnp.einsum(
        "bhqk,bkhd->bqhd", probabilities, value_pairs, preferred_element_type=jnp.float32
    )
    return attended.reshape(row_count, local_width)


def body(
    residual_in,
    query_rows,
    key_rows,
    value_rows,
    bc_weight,
    decay_rate,
    level_codes,
    level_scale,
    positions,
    ssm_gain,
):
    row_count, local_width = residual_in.shape
    edge_rows = from_behind(
        (key_rows[row_count - WINDOW :], value_rows[row_count - WINDOW :]), ("seq", "fsdp"), 1
    )
    attended = window_attention(
        query_rows, key_rows, value_rows, edge_rows[0], edge_rows[1], positions
    )
    hidden = (residual_in.astype(jnp.float32) + attended).astype(jnp.bfloat16)
    partial_value = jnp.dot(
        hidden,
        lax.all_gather(bc_weight, "fsdp", axis=0, tiled=True),
        preferred_element_type=jnp.float32,
    )
    bc_full = lax.psum(partial_value, "head").astype(jnp.bfloat16)
    b_mat = bc_full[:, :STATES]
    c_mat = bc_full[:, STATES:]
    ssm_count = decay_rate.shape[1]
    values_h = hidden.reshape(row_count, ssm_count, HEAD_VALUES)
    log_cum = -jnp.cumsum(decay_rate, axis=0)
    log_end = log_cum[row_count - 1]
    scaled = (
        jnp.exp(log_end[None, :] - log_cum)[:, :, None] * values_h.astype(jnp.float32)
    ).astype(jnp.bfloat16)
    block_state = lax.dot_general(
        b_mat,
        scaled.reshape(row_count, local_width),
        (((0,), (0,)), ((), ())),
        preferred_element_type=jnp.float32,
    )
    lambdas = level_codes.astype(jnp.float32) * level_scale[None, :]
    local_bits = row_count.bit_length() - 1
    token_index = jnp.arange(row_count, dtype=jnp.int32)
    xor_idx = jnp.bitwise_xor(token_index[:, None], token_index[None, :])
    causal = token_index[None, :] <= token_index[:, None]
    level_weight = jnp.zeros((row_count, row_count), jnp.float32)
    for level_idx in range(local_bits + 1):
        low_edge = 0 if level_idx == 0 else 1 << level_idx - 1
        high_edge = 1 << level_idx
        inside = (xor_idx >= low_edge) & (xor_idx < high_edge)
        level_weight = level_weight + jnp.where(inside, lambdas[:, level_idx : level_idx + 1], 0.0)
    gram_mat = lax.dot_general(
        c_mat, b_mat, (((1,), (1,)), ((), ())), preferred_element_type=jnp.float32
    )
    shared = jnp.where(causal, gram_mat * level_weight, 0.0)

    def head_term(operands):
        cum_head, values_head = operands
        decay_mat = jnp.exp(jnp.where(causal, cum_head[:, None] - cum_head[None, :], -jnp.inf))
        mixing = (shared * decay_mat).astype(jnp.bfloat16)
        return jnp.dot(mixing, values_head, preferred_element_type=jnp.float32)

    intra_term = lax.map(head_term, (log_cum.T, jnp.transpose(values_h, (1, 0, 2))))
    shard_count = lax.axis_size(("seq", "fsdp"))
    shard_pos = lax.axis_index(("seq", "fsdp"))
    cross_count = shard_count.bit_length() - 1
    carry_state = block_state
    carry_end = log_end
    before = jnp.zeros_like(log_end)
    carried_list = []
    for bit_pos in range(cross_count):
        other_state, other_end = partner((carry_state, carry_end), ("seq", "fsdp"), bit_pos)
        upper_half = jnp.bitwise_and(jnp.right_shift(shard_pos, bit_pos), 1) == 1
        carried_list.append(
            jnp.where(upper_half, other_state * widen(jnp.exp(before), HEAD_VALUES)[None, :], 0.0)
        )
        joined_upper = other_state * widen(jnp.exp(carry_end), HEAD_VALUES)[None, :] + carry_state
        joined_lower = carry_state * widen(jnp.exp(other_end), HEAD_VALUES)[None, :] + other_state
        carry_state = jnp.where(upper_half, joined_upper, joined_lower)
        before = jnp.where(upper_half, before + other_end, before)
        carry_end = carry_end + other_end
    levels_state = jnp.stack(carried_list, axis=0)
    stacked = jnp.transpose(levels_state.astype(jnp.bfloat16), (1, 0, 2)).reshape(
        STATES, cross_count * local_width
    )
    level_reads = jnp.dot(c_mat, stacked, preferred_element_type=jnp.float32).reshape(
        row_count, cross_count, ssm_count, HEAD_VALUES
    )
    lam_cross = lambdas[:, local_bits + 1 : local_bits + 1 + cross_count]
    cross_term = jnp.einsum("rl,rlhp->rhp", lam_cross, level_reads) * jnp.exp(log_cum)[:, :, None]
    ssm_out = jnp.transpose(intra_term, (1, 0, 2)) + cross_term
    inv_rms = lax.rsqrt(jnp.mean(ssm_out * ssm_out, axis=2, keepdims=True) + 1e-05)
    result = (
        hidden.astype(jnp.float32)
        + (ssm_out * inv_rms).reshape(row_count, local_width) * ssm_gain[None, :]
    )
    return result.astype(jnp.bfloat16)


def solution(mesh):
    in_specs = (
        P(("groups", "seq", "fsdp"), "head"),
        P(("groups", "seq", "fsdp"), "head"),
        P(("groups", "seq", "fsdp"), "head"),
        P(("groups", "seq", "fsdp"), "head"),
        P(("head", "fsdp"), None),
        P(("groups", "seq", "fsdp"), "head"),
        P(("groups", "seq", "fsdp"), None),
        P(),
        P(("groups", "seq", "fsdp")),
        P("head"),
    )
    out_specs = P(("groups", "seq", "fsdp"), "head")
    return jax.shard_map(body, mesh=mesh, in_specs=in_specs, out_specs=out_specs, check_vma=False)
```

profile of v0, /device:TPU:0, one launch (start us, length us, event | category | flops | bytes accessed | tf_op | source)
XLA Modules:
  0.0 232.8 jit_solution(9729053218725581105)
XLA Ops:
  0.9 4.5 %reduce-window.6 = f32[16,8,128]{2,1,0:T(8,128)S(1)} reduce-window(f32[16,8,128]{2,1,0:T(8,128)S(1)} %bitcast.138, f32[]{:T(128)} %constant.32.clone.1), window={size=1x1x128 pad=0_0x0_0x127_0}, to_apply=%region_2.3 | reduce-window | flops 2080768 | bytes 131076 | tf_op jit(solution)/shard_map/reduce-window
  8.7 1.9 collective-permute-start.1
  12.3 4.6 %collective-permute-start = (bf16[128,1024]{1,0:T(8,128)(2,1)}, bf16[128,1024]{1,0:T(8,128)(2,1)S(1)}, u32[]{:S(2)}, u32[]{:S(2)}) collective-permute-start(bf16[128,1024]{1,0:T(8,128)(2,1)} %slice.77), channel_id=1, source_target_pairs={{0,1},{1,4},{4,5},{5,8},{8,9},{9,12},{12,13},{2,3},{3,6},{6,7},{7,... | collective-permute-start | bytes 786440 | tf_op jit(solution)/shard_map/ppermute | solution.py:17
  17.8 2.4 %copy.58 = bf16[128,8,8,128]{3,2,1,0:T(8,128)(2,1)S(1)} copy(bf16[128,8,8,128]{3,1,2,0:T(8,128)(2,1)} %bitcast.126) | data formatting | bytes 4194304
  20.1 1.9 copy.35
  22.0 1.9 copy.59
  24.0 2.0 copy.56
  26.0 4.1 %copy.33 = bf16[8,128,8,128]{1,3,2,0:T(8,128)(2,1)} copy(bf16[8,128,8,128]{3,2,1,0:T(8,128)(2,1)} %bitcast.132) | data formatting | bytes 4194304 | tf_op jit(solution)/shard_map/slice | solution.py:39
  30.1 2.5 %mul.119 = f32[1024,16,64]{0,2,1:T(8,128)} broadcast(f32[1024,16]{0,1:T(8,128)S(1)} %get-tuple-element.85), dimensions={0,1} | broadcast | bytes 4259840 | tf_op jit(solution)/shard_map/mul | solution.py:96
  32.6 5.5 %copy.43 = f32[1024,1024]{1,0:T(8,128)} copy(f32[1024,1024]{0,1:T(8,128)} %bitcast.124) | data formatting | bytes 8388608 | tf_op jit(solution)/shard_map/mul | solution.py:96
  39.7 2.3 all_gather.3
  42.8 1.9 copy.34
  44.9 2.0 copy.55
  46.9 4.1 %copy.32 = bf16[8,128,8,128]{1,3,2,0:T(8,128)(2,1)} copy(bf16[8,128,8,128]{3,2,1,0:T(8,128)(2,1)} %bitcast.130) | data formatting | bytes 4194304 | tf_op jit(solution)/shard_map/slice | solution.py:39
  51.0 3.5 %fusion.19 = f32[8,8,256,128]{3,2,1,0:T(8,128)S(1)} fusion(bf16[8,128,8,128]{3,1,2,0:T(8,128)(2,1)S(1)} %copy-done.4, bf16[8,128,8,128]{3,1,2,0:T(8,128)(2,1)} %copy.34, bf16[8,128,8,128]{3,2,1,0:T(8,128)(2,1)} %bitcast.128), kind=kOutput, calls=%fused_computation.28 | convolution fusion | flops 545259520 | bytes 14680064 | tf_op jit(solution)/shard_map/bqhd,bkhd->bhqk/dot_general | solution.py:41
  54.6 4.4 %fusion.85 = (f32[8,8,128]{2,1,0:T(8,128)S(1)}, f32[8,8,128,256]{2,3,1,0:T(8,128)}) fusion(f32[8,8,256,128]{3,2,1,0:T(8,128)S(1)} %fusion.19, pred[8,128,256]{1,2,0:T(8,128)(4,1)S(1)} %copy-done.9), kind=kOutput, calls=%fused_computation.118 | output fusion | flops 12583167 | bytes 17072128 | tf_op jit(solution)/shard_map/sub | solution.py:55
  59.0 6.6 %fusion.59 = f32[8,128,8,128]{1,3,2,0:T(8,128)} fusion(f32[8,8,128,256]{2,3,1,0:T(8,128)} %get-tuple-element.95, f32[8,8,128]{2,1,0:T(8,128)S(1)} %get-tuple-element.94, bf16[8,128,8,128]{1,3,2,0:T(8,128)(2,1)S(1)} %copy-done.6, bf16[8,128,8,128]{1,3,2,0:T(8,128)(2,1)S(1)} %copy-done.7), kind=kOutput, calls=%fused_computation.73 | convolution fusion | flops 549453824 | bytes 16809984 | tf_op jit(solution)/shard_map/bhqk,bkhd->bqhd/dot_general | solution.py:57
  65.6 5.3 %copy.38 = f32[8,128,8,128]{3,2,1,0:T(8,128)} copy(f32[8,128,8,128]{1,3,2,0:T(8,128)} %fusion.59) | data formatting | bytes 8388608 | tf_op jit(solution)/shard_map/bhqk,bkhd->bqhd/transpose | solution.py:57
  71.0 4.0 %fusion.14 = bf16[1024,1024]{1,0:T(8,128)(2,1)S(1)} fusion(f32[128,8,8,128]{3,2,1,0:T(8,128)} %bitcast.125, bf16[1024,1024]{1,0:T(8,128)(2,1)} %param.12), kind=kLoop, calls=%fused_computation.23 | loop fusion | flops 3145728 | bytes 8388608 | tf_op jit(solution)/shard_map/convert_element_type | solution.py:82
  76.7 30.9 %all-reduce.1 = bf16[1024,256]{1,0:T(8,128)(2,1)S(1)} all-reduce(f32[1024,256]{1,0:T(8,128)} %fusion.86), channel_id=1, replica_groups=mesh['groups'=2,'seq'=4,'head'=2,'fsdp'=2] {'head'}, use_global_device_ids=true, to_apply=%region_4.5 | all-reduce | flops 262144 | bytes 1572864 | tf_op jit(solution)/shard_map/psum | solution.py:88
  107.6 2.7 %fusion.62 = f32[128,1024]{1,0:T(8,128)S(1)} fusion(f32[1024,1024]{1,0:T(8,128)} %copy.43, bf16[1024,1024]{1,0:T(8,128)(2,1)S(1)} %fusion.14, bf16[1024,256]{1,0:T(8,128)(2,1)S(1)} %all-reduce.1), kind=kOutput, calls=%fused_computation.74 | convolution fusion | flops 271581184 | bytes 7077888 | tf_op jit(solution)/shard_map/dot_general | solution.py:98
  118.4 2.0 add_select_fusion.1
  121.9 10.7 %multiply_select_fusion = f32[1024,1024]{1,0:T(8,128)} fusion(f32[1024]{0:T(1024)} %bitcast.146, f32[1024]{0:T(1024)} %bitcast.147, f32[1024]{0:T(1024)} %bitcast.148, f32[1024]{0:T(1024)} %bitcast.149, f32[1024]{0:T(1024)} %bitcast.150, f32[1024]{0:T(1024)} %bitcast.151, f32[1024]{0:T(1024)} %bitcast.152, f32[1024]{0:T(1024)} %bitcast.153, ...), kind=kOutput, calls=%fused_computation.34 | convolution fusion | flops 329252864 | bytes 4763648 | tf_op jit(solution)/shard_map/dot_general | solution.py:115
  132.5 2.6 %copy.41 = bf16[1024,1024]{0,1:T(8,128)(2,1)} copy(bf16[1024,1024]{1,0:T(8,128)(2,1)S(1)} %fusion.14) | data formatting | bytes 4194304 | tf_op jit(solution)/shard_map/convert_element_type | solution.py:82
  135.1 2.0 fusion.68
  138.3 61.2 %while.11 = (s32[]{:T(128)}, f32[16,1024,64]{1,2,0:T(8,128)}, f32[16,1024]{1,0:T(8,128)S(1)}, f32[1024,1024]{1,0:T(8,128)}, bf16[16,1024,64]{1,2,0:T(8,128)(2,1)}, /*index=5*/s32[]{:T(128)}) while((s32[]{:T(128)}, f32[16,1024,64]{1,2,0:T(8,128)}, f32[16,1024]{1,0:T(8,128)S(1)}, f32[1024,1024]{1,0:T(8,128)}, ...), condition=%wide.region_6.7_spmd.clone, body=%wide.region_5.6_spmd.clone.sunk | while | flops 139460608 | bytes 4605001 | solution.py:126
  138.3 3.8 %fusion.93 = f32[16,1024,64]{1,2,0:T(8,128)} fusion(f32[16,1024,64]{1,2,0:T(8,128)} %get-tuple-element.134, s32[]{:T(128)} %get-tuple-element.133, f32[1024,1024]{1,0:T(8,128)} %get-tuple-element.142, f32[1024]{0:T(1024)S(1)} %bitcast.141, bf16[16,1024,64]{1,2,0:T(8,128)(2,1)} %get-tuple-element.143), kind=kOutput, calls=%fused_computation.5.clone.1 | convolution fusion | flops 139460608 | bytes 4596736 | tf_op jit(solution)/shard_map/while/body/eval_jaxpr/dot_general | solution.py:124
  142.1 3.8 %fusion.93 = f32[16,1024,64]{1,2,0:T(8,128)} fusion(f32[16,1024,64]{1,2,0:T(8,128)} %get-tuple-element.134, s32[]{:T(128)} %get-tuple-element.133, f32[1024,1024]{1,0:T(8,128)} %get-tuple-element.142, f32[1024]{0:T(1024)S(1)} %bitcast.141, bf16[16,1024,64]{1,2,0:T(8,128)(2,1)} %get-tuple-element.143), kind=kOutput, calls=%fused_computation.5.clone.1 | convolution fusion | flops 139460608 | bytes 4596736 | tf_op jit(solution)/shard_map/while/body/eval_jaxpr/dot_general | solution.py:124
  146.0 3.8 %fusion.93 = f32[16,1024,64]{1,2,0:T(8,128)} fusion(f32[16,1024,64]{1,2,0:T(8,128)} %get-tuple-element.134, s32[]{:T(128)} %get-tuple-element.133, f32[1024,1024]{1,0:T(8,128)} %get-tuple-element.142, f32[1024]{0:T(1024)S(1)} %bitcast.141, bf16[16,1024,64]{1,2,0:T(8,128)(2,1)} %get-tuple-element.143), kind=kOutput, calls=%fused_computation.5.clone.1 | convolution fusion | flops 139460608 | bytes 4596736 | tf_op jit(solution)/shard_map/while/body/eval_jaxpr/dot_general | solution.py:124
  149.8 3.8 %fusion.93 = f32[16,1024,64]{1,2,0:T(8,128)} fusion(f32[16,1024,64]{1,2,0:T(8,128)} %get-tuple-element.134, s32[]{:T(128)} %get-tuple-element.133, f32[1024,1024]{1,0:T(8,128)} %get-tuple-element.142, f32[1024]{0:T(1024)S(1)} %bitcast.141, bf16[16,1024,64]{1,2,0:T(8,128)(2,1)} %get-tuple-element.143), kind=kOutput, calls=%fused_computation.5.clone.1 | convolution fusion | flops 139460608 | bytes 4596736 | tf_op jit(solution)/shard_map/while/body/eval_jaxpr/dot_general | solution.py:124
  153.6 3.8 %fusion.93 = f32[16,1024,64]{1,2,0:T(8,128)} fusion(f32[16,1024,64]{1,2,0:T(8,128)} %get-tuple-element.134, s32[]{:T(128)} %get-tuple-element.133, f32[1024,1024]{1,0:T(8,128)} %get-tuple-element.142, f32[1024]{0:T(1024)S(1)} %bitcast.141, bf16[16,1024,64]{1,2,0:T(8,128)(2,1)} %get-tuple-element.143), kind=kOutput, calls=%fused_computation.5.clone.1 | convolution fusion | flops 139460608 | bytes 4596736 | tf_op jit(solution)/shard_map/while/body/eval_jaxpr/dot_general | solution.py:124
  157.5 3.8 %fusion.93 = f32[16,1024,64]{1,2,0:T(8,128)} fusion(f32[16,1024,64]{1,2,0:T(8,128)} %get-tuple-element.134, s32[]{:T(128)} %get-tuple-element.133, f32[1024,1024]{1,0:T(8,128)} %get-tuple-element.142, f32[1024]{0:T(1024)S(1)} %bitcast.141, bf16[16,1024,64]{1,2,0:T(8,128)(2,1)} %get-tuple-element.143), kind=kOutput, calls=%fused_computation.5.clone.1 | convolution fusion | flops 139460608 | bytes 4596736 | tf_op jit(solution)/shard_map/while/body/eval_jaxpr/dot_general | solution.py:124
  161.3 3.8 %fusion.93 = f32[16,1024,64]{1,2,0:T(8,128)} fusion(f32[16,1024,64]{1,2,0:T(8,128)} %get-tuple-element.134, s32[]{:T(128)} %get-tuple-element.133, f32[1024,1024]{1,0:T(8,128)} %get-tuple-element.142, f32[1024]{0:T(1024)S(1)} %bitcast.141, bf16[16,1024,64]{1,2,0:T(8,128)(2,1)} %get-tuple-element.143), kind=kOutput, calls=%fused_computation.5.clone.1 | convolution fusion | flops 139460608 | bytes 4596736 | tf_op jit(solution)/shard_map/while/body/eval_jaxpr/dot_general | solution.py:124
  165.1 3.8 %fusion.93 = f32[16,1024,64]{1,2,0:T(8,128)} fusion(f32[16,1024,64]{1,2,0:T(8,128)} %get-tuple-element.134, s32[]{:T(128)} %get-tuple-element.133, f32[1024,1024]{1,0:T(8,128)} %get-tuple-element.142, f32[1024]{0:T(1024)S(1)} %bitcast.141, bf16[16,1024,64]{1,2,0:T(8,128)(2,1)} %get-tuple-element.143), kind=kOutput, calls=%fused_computation.5.clone.1 | convolution fusion | flops 139460608 | bytes 4596736 | tf_op jit(solution)/shard_map/while/body/eval_jaxpr/dot_general | solution.py:124
  168.9 3.8 %fusion.93 = f32[16,1024,64]{1,2,0:T(8,128)} fusion(f32[16,1024,64]{1,2,0:T(8,128)} %get-tuple-element.134, s32[]{:T(128)} %get-tuple-element.133, f32[1024,1024]{1,0:T(8,128)} %get-tuple-element.142, f32[1024]{0:T(1024)S(1)} %bitcast.141, bf16[16,1024,64]{1,2,0:T(8,128)(2,1)} %get-tuple-element.143), kind=kOutput, calls=%fused_computation.5.clone.1 | convolution fusion | flops 139460608 | bytes 4596736 | tf_op jit(solution)/shard_map/while/body/eval_jaxpr/dot_general | solution.py:124
  172.7 3.8 %fusion.93 = f32[16,1024,64]{1,2,0:T(8,128)} fusion(f32[16,1024,64]{1,2,0:T(8,128)} %get-tuple-element.134, s32[]{:T(128)} %get-tuple-element.133, f32[1024,1024]{1,0:T(8,128)} %get-tuple-element.142, f32[1024]{0:T(1024)S(1)} %bitcast.141, bf16[16,1024,64]{1,2,0:T(8,128)(2,1)} %get-tuple-element.143), kind=kOutput, calls=%fused_computation.5.clone.1 | convolution fusion | flops 139460608 | bytes 4596736 | tf_op jit(solution)/shard_map/while/body/eval_jaxpr/dot_general | solution.py:124
  176.6 3.8 %fusion.93 = f32[16,1024,64]{1,2,0:T(8,128)} fusion(f32[16,1024,64]{1,2,0:T(8,128)} %get-tuple-element.134, s32[]{:T(128)} %get-tuple-element.133, f32[1024,1024]{1,0:T(8,128)} %get-tuple-element.142, f32[1024]{0:T(1024)S(1)} %bitcast.141, bf16[16,1024,64]{1,2,0:T(8,128)(2,1)} %get-tuple-element.143), kind=kOutput, calls=%fused_computation.5.clone.1 | convolution fusion | flops 139460608 | bytes 4596736 | tf_op jit(solution)/shard_map/while/body/eval_jaxpr/dot_general | solution.py:124
  180.4 3.8 %fusion.93 = f32[16,1024,64]{1,2,0:T(8,128)} fusion(f32[16,1024,64]{1,2,0:T(8,128)} %get-tuple-element.134, s32[]{:T(128)} %get-tuple-element.133, f32[1024,1024]{1,0:T(8,128)} %get-tuple-element.142, f32[1024]{0:T(1024)S(1)} %bitcast.141, bf16[16,1024,64]{1,2,0:T(8,128)(2,1)} %get-tuple-element.143), kind=kOutput, calls=%fused_computation.5.clone.1 | convolution fusion | flops 139460608 | bytes 4596736 | tf_op jit(solution)/shard_map/while/body/eval_jaxpr/dot_general | solution.py:124
  184.2 3.8 %fusion.93 = f32[16,1024,64]{1,2,0:T(8,128)} fusion(f32[16,1024,64]{1,2,0:T(8,128)} %get-tuple-element.134, s32[]{:T(128)} %get-tuple-element.133, f32[1024,1024]{1,0:T(8,128)} %get-tuple-element.142, f32[1024]{0:T(1024)S(1)} %bitcast.141, bf16[16,1024,64]{1,2,0:T(8,128)(2,1)} %get-tuple-element.143), kind=kOutput, calls=%fused_computation.5.clone.1 | convolution fusion | flops 139460608 | bytes 4596736 | tf_op jit(solution)/shard_map/while/body/eval_jaxpr/dot_general | solution.py:124
  188.1 3.8 %fusion.93 = f32[16,1024,64]{1,2,0:T(8,128)} fusion(f32[16,1024,64]{1,2,0:T(8,128)} %get-tuple-element.134, s32[]{:T(128)} %get-tuple-element.133, f32[1024,1024]{1,0:T(8,128)} %get-tuple-element.142, f32[1024]{0:T(1024)S(1)} %bitcast.141, bf16[16,1024,64]{1,2,0:T(8,128)(2,1)} %get-tuple-element.143), kind=kOutput, calls=%fused_computation.5.clone.1 | convolution fusion | flops 139460608 | bytes 4596736 | tf_op jit(solution)/shard_map/while/body/eval_jaxpr/dot_general | solution.py:124
  191.9 3.8 %fusion.93 = f32[16,1024,64]{1,2,0:T(8,128)} fusion(f32[16,1024,64]{1,2,0:T(8,128)} %get-tuple-element.134, s32[]{:T(128)} %get-tuple-element.133, f32[1024,1024]{1,0:T(8,128)} %get-tuple-element.142, f32[1024]{0:T(1024)S(1)} %bitcast.141, bf16[16,1024,64]{1,2,0:T(8,128)(2,1)} %get-tuple-element.143), kind=kOutput, calls=%fused_computation.5.clone.1 | convolution fusion | flops 139460608 | bytes 4596736 | tf_op jit(solution)/shard_map/while/body/eval_jaxpr/dot_general | solution.py:124
  195.7 3.8 %fusion.93 = f32[16,1024,64]{1,2,0:T(8,128)} fusion(f32[16,1024,64]{1,2,0:T(8,128)} %get-tuple-element.134, s32[]{:T(128)} %get-tuple-element.133, f32[1024,1024]{1,0:T(8,128)} %get-tuple-element.142, f32[1024]{0:T(1024)S(1)} %bitcast.141, bf16[16,1024,64]{1,2,0:T(8,128)(2,1)} %get-tuple-element.143), kind=kOutput, calls=%fused_computation.5.clone.1 | convolution fusion | flops 139460608 | bytes 4596736 | tf_op jit(solution)/shard_map/while/body/eval_jaxpr/dot_general | solution.py:124
  203.2 6.3 %fusion.70 = f32[1024,3,16,64]{0,3,2,1:T(8,128)} fusion(bf16[3,16,64,128]{3,2,1,0:T(8,128)(2,1)S(1)} %bitcast.133, bf16[1024,256]{1,0:T(8,128)(2,1)S(1)} %all-reduce.1), kind=kOutput, calls=%fused_computation.91 | convolution fusion | flops 805306368 | bytes 13631488 | tf_op jit(solution)/shard_map/dot_general | solution.py:149
  209.5 6.9 %fusion.10 = f32[1024,1024]{0,1:T(8,128)S(1)} fusion(f32[1024,3,16,64]{0,3,2,1:T(8,128)} %fusion.70, f32[1024,3]{0,1:T(4,128)S(1)} %slice.117), kind=kLoop, calls=%fused_computation.13 | loop fusion | flops 5242880 | bytes 16789504
  216.4 3.6 %multiply_reduce_fusion = f32[1024,16]{0,1:T(8,128)S(1)} fusion(f32[1024,16]{0,1:T(8,128)S(1)} %get-tuple-element.86, f32[16,1024,64]{1,2,0:T(8,128)} %get-tuple-element.37, f32[1024,1024]{0,1:T(8,128)S(1)} %fusion.10), kind=kLoop, calls=%fused_computation.33 | loop fusion | flops 4177920 | bytes 8519680 | tf_op jit(solution)/shard_map/reduce_sum | solution.py:155
  220.0 3.1 %broadcast_multiply_fusion = f32[1024,16,64]{0,2,1:T(8,128)} fusion(f32[1024,16]{0,1:T(8,128)S(1)} %add_rsqrt_fusion, f32[1024,16]{0,1:T(8,128)S(1)} %get-tuple-element.86, f32[16,1024,64]{1,2,0:T(8,128)S(1)} %copy-done, f32[1024,1024]{0,1:T(8,128)S(1)} %fusion.10), kind=kLoop, calls=%fused_computation.80 | loop fusion | flops 3145728 | bytes 12713984 | tf_op jit(solution)/shard_map/mul | solution.py:158
  223.1 5.4 %copy.45 = f32[1024,1024]{1,0:T(8,128)} copy(f32[1024,1024]{0,1:T(8,128)} %bitcast.123) | data formatting | bytes 8388608 | tf_op jit(solution)/shard_map/reshape | solution.py:158
  228.5 4.3 %fusion.13 = bf16[1024,1024]{1,0:T(8,128)(2,1)} fusion(bf16[1024,1024]{1,0:T(8,128)(2,1)S(1)} %fusion.14, f32[1024,1024]{1,0:T(8,128)} %copy.45, f32[1024]{0:T(1024)S(1)} %copy-done.13), kind=kLoop, calls=%fused_computation.21 | loop fusion | flops 4194304 | bytes 8392704 | tf_op jit(solution)/shard_map/convert_element_type | solution.py:160
  (101 shorter events, 25.5 us)
Async XLA Ops:
  6.6 104.5 %collective-permute-start.3 = (f32[16]{0:T(128)}, f32[16]{0:T(128)}, u32[]{:S(2)}, u32[]{:S(2)}) collective-permute-start(f32[16]{0:T(128)} %slice_reduce_fusion), channel_id=1, source_target_pairs={{0,1},{1,0},{4,5},{5,4},{8,9},{9,8},{12,13},{13,12},{2,3},{3,2},{6... | collective-permute-start | bytes 200 | tf_op jit(solution)/shard_map/ppermute | solution.py:21
  8.7 33.3 %collective-permute-start.1 = (bf16[128,1024]{1,0:T(8,128)(2,1)}, bf16[128,1024]{1,0:T(8,128)(2,1)S(1)}, u32[]{:S(2)}, u32[]{:S(2)}) collective-permute-start(bf16[128,1024]{1,0:T(8,128)(2,1)} %slice.81), channel_id=1, source_target_pairs={{0,1},{1,4},{4,5},{5,8},{8,9},{9,12},{12,13},{2,3},{3,6},{6,7},{7,... | collective-permute-start | bytes 786440 | tf_op jit(solution)/shard_map/ppermute | solution.py:17
  12.3 32.4 %collective-permute-start = (bf16[128,1024]{1,0:T(8,128)(2,1)}, bf16[128,1024]{1,0:T(8,128)(2,1)S(1)}, u32[]{:S(2)}, u32[]{:S(2)}) collective-permute-start(bf16[128,1024]{1,0:T(8,128)(2,1)} %slice.77), channel_id=1, source_target_pairs={{0,1},{1,4},{4,5},{5,8},{8,9},{9,12},{12,13},{2,3},{3,6},{6,7},{7,... | collective-permute-start | bytes 786440 | tf_op jit(solution)/shard_map/ppermute | solution.py:17
  17.7 4.3 %copy-start.5 = (bf16[1024,1024]{1,0:T(8,128)(2,1)S(1)}, bf16[1024,1024]{1,0:T(8,128)(2,1)}, u32[]{:S(2)}) copy-start(bf16[1024,1024]{1,0:T(8,128)(2,1)} %param.13) | copy-start | bytes 6291460
  20.1 3.9 %copy-start.2 = (bf16[1024,1024]{1,0:T(8,128)(2,1)S(1)}, bf16[1024,1024]{1,0:T(8,128)(2,1)}, u32[]{:S(2)}) copy-start(bf16[1024,1024]{1,0:T(8,128)(2,1)} %param.15) | copy-start | bytes 6291460
  32.5 5.5 %copy-start.12 = (s32[1024]{0:T(1024)S(1)}, s32[1024]{0:T(1024)}, u32[]{:S(2)}) copy-start(s32[1024]{0:T(1024)} %param.20) | copy-start | bytes 12292
  32.5 6.4 %copy-start.11 = (s32[1024,18]{0,1:T(8,128)S(1)}, s32[1024,18]{0,1:T(8,128)}, u32[]{:S(2)}) copy-start(s32[1024,18]{0,1:T(8,128)} %param.18) | copy-start | bytes 221188
  32.5 6.4 %copy-start.14 = (f32[18]{0:T(128)S(1)}, f32[18]{0:T(128)}, u32[]{:S(2)}) copy-start(f32[18]{0:T(128)} %param.19) | copy-start | bytes 220
  32.5 7.2 %copy-start.8 = (bf16[512,256]{1,0:T(8,128)(2,1)S(1)}, bf16[512,256]{1,0:T(8,128)(2,1)}, u32[]{:S(2)}) copy-start(bf16[512,256]{1,0:T(8,128)(2,1)} %param.16) | copy-start | bytes 786436
  32.5 9.4 %copy-start.1 = (bf16[1024,1024]{1,0:T(8,128)(2,1)S(1)}, bf16[1024,1024]{1,0:T(8,128)(2,1)}, u32[]{:S(2)}) copy-start(bf16[1024,1024]{1,0:T(8,128)(2,1)} %param.14) | copy-start | bytes 6291460
  42.2 2.6 %copy-start.3 = (bf16[1024,1024]{1,0:T(8,128)(2,1)S(1)}, bf16[1024,1024]{1,0:T(8,128)(2,1)}, u32[]{:S(2)}) copy-start(bf16[1024,1024]{1,0:T(8,128)(2,1)} %param.15) | copy-start | bytes 6291460
  44.9 6.1 %copy-start.4 = (bf16[8,128,8,128]{3,1,2,0:T(8,128)(2,1)S(1)}, bf16[8,128,8,128]{3,1,2,0:T(8,128)(2,1)}, u32[]{:S(2)}) copy-start(bf16[8,128,8,128]{3,1,2,0:T(8,128)(2,1)} %copy.35) | copy-start | bytes 6291460
  51.0 3.5 %copy-start.9 = (pred[8,128,256]{1,2,0:T(8,128)(4,1)S(1)}, pred[8,128,256]{1,2,0:T(8,128)(4,1)}, u32[]{:S(2)}) copy-start(pred[8,128,256]{1,2,0:T(8,128)(4,1)} %compare_and_fusion) | copy-start | bytes 786436
  54.6 4.4 %copy-start.6 = (bf16[8,128,8,128]{1,3,2,0:T(8,128)(2,1)S(1)}, bf16[8,128,8,128]{1,3,2,0:T(8,128)(2,1)}, u32[]{:S(2)}) copy-start(bf16[8,128,8,128]{1,3,2,0:T(8,128)(2,1)} %copy.33) | copy-start | bytes 6291460
  54.6 4.4 %copy-start.7 = (bf16[8,128,8,128]{1,3,2,0:T(8,128)(2,1)S(1)}, bf16[8,128,8,128]{1,3,2,0:T(8,128)(2,1)}, u32[]{:S(2)}) copy-start(bf16[8,128,8,128]{1,3,2,0:T(8,128)(2,1)} %copy.32) | copy-start | bytes 6291460
  76.7 33.7 %copy-start.10 = (f32[1024,18]{0,1:T(8,128)S(1)}, f32[1024,18]{0,1:T(8,128)}, u32[]{:S(2)}) copy-start(f32[1024,18]{0,1:T(8,128)} %convert_multiply_fusion.1) | copy-start | bytes 221188
  110.3 8.0 %collective-permute-start.2 = (f32[128,1024]{1,0:T(8,128)S(1)}, f32[128,1024]{1,0:T(8,128)}, u32[]{:S(2)}, u32[]{:S(2)}) collective-permute-start(f32[128,1024]{1,0:T(8,128)S(1)} %fusion.62), channel_id=1, source_target_pairs={{0,1},{1,0},{4,5},{5,4},{8,9},{9,8},{12,13},{13,12},{2,3},{3,2},{6... | collective-permute-start | bytes 1572872 | tf_op jit(solution)/shard_map/ppermute | solution.py:21
  111.8 3.6 %collective-permute-start.5 = (f32[16]{0:T(128)S(1)}, f32[16]{0:T(128)S(1)}, u32[]{:S(2)}, u32[]{:S(2)}) collective-permute-start(f32[16]{0:T(128)S(1)} %get-tuple-element.71), channel_id=1, source_target_pairs={{0,4},{1,5},{4,0},{5,1},{8,12},{9,13},{12,8},{13,9},{2,6},{3,7},{6... | collective-permute-start | bytes 200 | tf_op jit(solution)/shard_map/ppermute | solution.py:21
  120.3 14.8 %collective-permute-start.4 = (f32[128,1024]{1,0:T(8,128)}, f32[128,1024]{1,0:T(8,128)S(1)}, u32[]{:S(2)}, u32[]{:S(2)}) collective-permute-start(f32[128,1024]{1,0:T(8,128)} %add_select_fusion.1), channel_id=1, source_target_pairs={{0,4},{1,5},{4,0},{5,1},{8,12},{9,13},{12,8},{13,9},{2,6},{3,7},{6... | collective-permute-start | bytes 1572872 | tf_op jit(solution)/shard_map/ppermute | solution.py:21
  137.1 62.5 %collective-permute-start.6 = (f32[128,1024]{1,0:T(8,128)}, f32[128,1024]{1,0:T(8,128)}, u32[]{:S(2)}, u32[]{:S(2)}) collective-permute-start(f32[128,1024]{1,0:T(8,128)} %get-tuple-element.73), channel_id=1, source_target_pairs={{0,8},{1,9},{4,12},{5,13},{8,0},{9,1},{12,4},{13,5},{2,10},{3,11},... | collective-permute-start | bytes 1572872 | tf_op jit(solution)/shard_map/ppermute | solution.py:21
  216.4 3.6 %copy-start = (f32[16,1024,64]{1,2,0:T(8,128)S(1)}, f32[16,1024,64]{1,2,0:T(8,128)}, u32[]{:S(2)}) copy-start(f32[16,1024,64]{1,2,0:T(8,128)} %get-tuple-element.37) | copy-start | bytes 12582916
  223.1 5.4 %copy-start.13 = (f32[1024]{0:T(1024)S(1)}, f32[1024]{0:T(1024)}, u32[]{:S(2)}) copy-start(f32[1024]{0:T(1024)} %param.21) | copy-start | bytes 12292
where the time goes:
time: 234 us; the launch traced here: 233 us
  matrix products  92.7 us (40%)
  local copies, waits for them, and re-layouts  53 us (23%)
  other arithmetic  41 us (18%)
  blocking collectives  33.2 us (14%)
  starting transfers between devices  11.4 us (5%)
    dot_general x16, matrix products, head_term(): return jnp.dot(mixing, values_head, preferred_element_type=jnp.float32)  61.1 us
    psum x1, blocking collectives, body(): bc_full = lax.psum(partial_value, 'head').astype(jnp.bfloat16)  30.9 us
    dot_general x1, matrix products, body(): lax.dot_general(c_mat, b_mat, (((1,), (1,)), ((), ())), preferred_element...  10.7 us
    unnamed x37, local copies, waits for them, and re-layouts  9.81 us
    mul x2, local copies, waits for them, and re-layouts, body(): jnp.exp(log_end[None, :] - log_cum)[:, :, None]  7.98 us
    unnamed x3, other arithmetic  7.28 us
    dot_general x1, matrix products, window_attention(): jnp.einsum('bhqk,bkhd->bqhd', probabilities, value_pairs, preferred_eleme...  6.63 us
    ppermute x2, starting transfers between devices, from_behind(): return lax.ppermute(x, axis, pairs)  6.48 us
  transfers between devices with their start and end apart: 7, of which 1 were waited for; matrix products, arithmetic and copies ran while one was open for 61% of the time, Pallas kernels for 0%

commit v1 on v0

v1 whole, which is shorter than its diff:
```python
import functools
import math

import jax
import jax.numpy as jnp
from jax import lax
from jax.experimental import pallas as pl
from jax.experimental.pallas import tpu as pltpu
from jax.sharding import PartitionSpec as P

HEAD_DIM = 128
HEAD_VALUES = 64
STATES = 128
WINDOW = 128
CHUNK = 128
LOG2E = math.log2(math.e)
F32 = jnp.float32
BF16 = jnp.bfloat16


def iota(shape, axis):
    return lax.broadcasted_iota(jnp.int32, shape, axis)


def dot(a, b):
    return jnp.dot(a, b, preferred_element_type=F32)


def dot_nt(a, b):
    return lax.dot_general(a, b, (((1,), (1,)), ((), ())), preferred_element_type=F32)


def dot_tn(a, b):
    return lax.dot_general(a, b, (((0,), (0,)), ((), ())), preferred_element_type=F32)


def attention_kernel(q, kp, kc, vp, vc, ek, ev, pos, res, w, hid, part):
    first = pl.program_id(0) == 0
    width = q.shape[1]
    pos_col = jnp.broadcast_to(pos[0].astype(F32), (CHUNK, CHUNK)).T
    row = iota((CHUNK, CHUNK), 0)
    col = iota((CHUNK, CHUNK), 1)
    near = (row - col).astype(F32)
    far = near + float(WINDOW)
    mask_cur = jnp.where((near >= 0) & (near <= pos_col), 0.0, -jnp.inf)
    mask_prev = jnp.where((far < float(WINDOW)) & (far <= pos_col), 0.0, -jnp.inf)
    mask = jnp.concatenate([mask_prev, mask_cur], axis=1)
    scale = LOG2E / math.sqrt(HEAD_DIM)
    for h in range(width // HEAD_DIM):
        cols = slice(h * HEAD_DIM, (h + 1) * HEAD_DIM)
        k_prev = jnp.where(first, ek[:, cols], kp[:, cols])
        v_prev = jnp.where(first, ev[:, cols], vp[:, cols])
        keys = jnp.concatenate([k_prev, kc[:, cols]], axis=0)
        vals = jnp.concatenate([v_prev, vc[:, cols]], axis=0)
        s = dot_nt(q[:, cols], keys) + mask
        top = jnp.max(s, axis=1, keepdims=True)
        e = jnp.exp2((s - top) * scale)
        total = jnp.sum(e, axis=1, keepdims=True)
        att = dot(e.astype(BF16), vals) * (1.0 / total)
        hid[:, cols] = (res[:, cols].astype(F32) + att).astype(BF16)
    part[...] = dot(hid[...], w[...]).astype(BF16)


def attention(q, k, v, edge_k, edge_v, positions, res, w):
    rows, width = q.shape
    n = rows // CHUNK
    cur = pl.BlockSpec((CHUNK, width), lambda i: (i, 0))
    prev = pl.BlockSpec((CHUNK, width), lambda i: (jnp.maximum(i - 1, 0), 0))
    fixed = lambda a: pl.BlockSpec(a.shape, lambda i: (0,) * a.ndim)
    return pl.pallas_call(
        attention_kernel,
        grid=(n,),
        in_specs=[cur, prev, cur, prev, cur, fixed(edge_k), fixed(edge_v),
                  pl.BlockSpec((1, 1, CHUNK), lambda i: (i, 0, 0)), cur, fixed(w)],
        out_specs=[cur, pl.BlockSpec((CHUNK, w.shape[1]), lambda i: (i, 0))],
        out_shape=[jax.ShapeDtypeStruct((rows, width), BF16),
                   jax.ShapeDtypeStruct((rows, w.shape[1]), BF16)],
        name="window_attention",
    )(q, k, k, v, v, edge_k, edge_v, positions.reshape(n, 1, CHUNK), res, w)


def split2(x):
    hi = x.astype(BF16)
    lo = (x - hi.astype(F32)).astype(BF16)
    return jnp.concatenate([hi, lo], axis=1)


def spread_matrix(heads, width):
    same = iota((2 * heads, width), 0) % heads == iota((2 * heads, width), 1) // HEAD_VALUES
    return jnp.where(same, 1.0, 0.0).astype(BF16)


def chunk_decay(decay):
    tri = jnp.where(iota((CHUNK, CHUNK), 1) <= iota((CHUNK, CHUNK), 0), 1.0, 0.0)
    return jnp.dot(tri, decay * LOG2E, precision=lax.Precision.HIGHEST, preferred_element_type=F32)


def chunk_state(b, u, cum, spread):
    left = cum[CHUNK - 1 :, :] - cum
    scaled = dot(split2(jnp.exp2(-left)), spread) * u.astype(F32)
    return dot_tn(b, scaled.astype(BF16))


def state_kernel(hid, p0, p1, decay, spread, state, gone):
    @pl.when(pl.program_id(0) == 0)
    def _():
        state[...] = jnp.zeros_like(state)
        gone[...] = jnp.ones_like(gone)

    b = (p0[:, :STATES].astype(F32) + p1[:, :STATES].astype(F32)).astype(BF16)
    cum = chunk_decay(decay[...])
    d = dot(split2(jnp.exp2(-cum[CHUNK - 8 :, :])), spread[...])[7:8, :]
    state[...] = state[...] * d + chunk_state(b, hid[...], cum, spread[...])
    gone[...] = gone[...] * d


def block_state(hid, p0, p1, decay, spread):
    rows, width = hid.shape
    cur = lambda a: pl.BlockSpec((CHUNK, a.shape[1]), lambda i: (i, 0))
    fixed = lambda s: pl.BlockSpec(s, lambda i: (0, 0))
    return pl.pallas_call(
        state_kernel,
        grid=(rows // CHUNK,),
        in_specs=[cur(hid), cur(p0), cur(p1), cur(decay), fixed(spread.shape)],
        out_specs=[fixed((STATES, width)), fixed((1, width))],
        out_shape=[jax.ShapeDtypeStruct((STATES, width), F32), jax.ShapeDtypeStruct((1, width), F32)],
        name="block_state",
    )(hid, p0, p1, decay, spread)


def local_kernel(steps, hid, p0, p1, decay, codes, scale, spread, y, held):
    j = pl.program_id(0)
    width = hid.shape[1]
    pairs = width // CHUNK
    low_levels = CHUNK.bit_length()

    @pl.when(j == 0)
    def _():
        held[...] = jnp.zeros_like(held)

    bc = (p0[...].astype(F32) + p1[...].astype(F32)).astype(BF16)
    b, c = bc[:, :STATES], bc[:, STATES:]
    lam = codes[...].astype(F32) * scale[...]
    cum = chunk_decay(decay[...])
    cum_t = cum.T
    row = iota((CHUNK, CHUNK), 0)
    col = iota((CHUNK, CHUNK), 1)
    differ = row ^ col
    weight = jnp.broadcast_to(lam[:, 0:1], (CHUNK, CHUNK))
    for level in range(1, low_levels):
        weight = jnp.where(differ >= 1 << level - 1, lam[:, level : level + 1], weight)
    shared = jnp.where(col <= row, dot_nt(c, b) * weight, 0.0)
    c32 = c.astype(F32)
    reach = dot(split2(jnp.exp2(-cum)), spread[...])
    d = reach[CHUNK - 1 :, :]
    left_lane = iota((CHUNK, CHUNK), 1) < HEAD_VALUES
    if steps:
        reads = jnp.concatenate(
            [(c32 * lam[:, low_levels + s : low_levels + s + 1]).astype(BF16) for s in range(steps)], axis=1
        )
    for g in range(pairs):
        cols = slice(g * CHUNK, (g + 1) * CHUNK)
        u = hid[:, cols]
        zero = jnp.zeros_like(u)
        mixes = []
        for h in (2 * g, 2 * g + 1):
            gap = jnp.minimum(cum_t[h : h + 1, :] - cum[:, h : h + 1], 0.0)
            mixes.append((shared * jnp.exp2(gap)).astype(BF16))
        stack = jnp.concatenate([jnp.where(left_lane, u, zero), jnp.where(left_lane, zero, u)], axis=0)
        term = dot(jnp.concatenate(mixes, axis=1), stack)
        if steps:
            term += dot(reads, held[:, cols].astype(BF16)) * reach[:, cols]
        y[:, cols] = term
    if steps:
        total = chunk_state(b, hid[...], cum, spread[...])
        after = j + 1
        for s in range(steps):
            bit = (after >> s) & 1
            fresh = jnp.where((after & ((1 << s) - 1)) == 0, 1, 0)
            keep = (bit * (1 - fresh)).astype(F32)
            take = (bit * fresh).astype(F32)
            rows = slice(s * STATES, (s + 1) * STATES)
            moved = held[rows, :] * d
            held[rows, :] = moved * keep + total * take
            total += moved


def local_terms(hid, p0, p1, decay, codes, scale, spread):
    rows, width = hid.shape
    n = rows // CHUNK
    steps = n.bit_length() - 1
    cur = lambda a: pl.BlockSpec((CHUNK, a.shape[1]), lambda i: (i, 0))
    fixed = lambda s: pl.BlockSpec(s, lambda i: (0, 0))
    return pl.pallas_call(
        functools.partial(local_kernel, steps),
        grid=(n,),
        in_specs=[cur(hid), cur(p0), cur(p1), cur(decay), cur(codes), fixed(scale.shape), fixed(spread.shape)],
        out_specs=cur(hid),
        out_shape=jax.ShapeDtypeStruct((rows, width), F32),
        scratch_shapes=[pltpu.VMEM((max(steps, 1) * STATES, width), F32)],
        name="local_terms",
        cost_estimate=pl.CostEstimate(flops=2 * rows * width * 1024, bytes_accessed=8 * rows * width, transcendentals=0),
    )(hid, p0, p1, decay, codes, scale, spread)


def finish_kernel(first_level, cross, hid, p0, p1, decay, codes, scale, spread, y, carried, gain, out, past):
    width = hid.shape[1]

    @pl.when(pl.program_id(0) == 0)
    def _():
        past[...] = jnp.ones_like(past)

    lam = codes[...].astype(F32) * scale[...]
    cum = chunk_decay(decay[...])
    reach = dot(split2(jnp.exp2(-cum)), spread[...])
    c = (p0[:, STATES:].astype(F32) + p1[:, STATES:].astype(F32)).astype(BF16).astype(F32)
    reads = jnp.concatenate(
        [(c * lam[:, first_level + s : first_level + s + 1]).astype(BF16) for s in range(cross)], axis=1
    )
    side = (CHUNK, CHUNK)
    group = jnp.where(iota(side, 0) // HEAD_VALUES == iota(side, 1) // HEAD_VALUES, 1.0 / HEAD_VALUES, 0.0).astype(BF16)
    for g in range(width // CHUNK):
        cols = slice(g * CHUNK, (g + 1) * CHUNK)
        term = y[:, cols] + dot(reads, carried[:, cols]) * (reach[:, cols] * past[:, cols])
        mean = dot((term * term).astype(BF16), group)
        out[:, cols] = (
            hid[:, cols].astype(F32) + term * lax.rsqrt(mean + 1e-05) * gain[:, cols]
        ).astype(BF16)
    past[...] = past[...] * reach[CHUNK - 1 :, :]


def finish(first_level, cross, hid, p0, p1, decay, codes, scale, spread, y, carried, gain):
    rows, width = hid.shape
    cur = lambda a: pl.BlockSpec((CHUNK, a.shape[1]), lambda i: (i, 0))
    fixed = lambda s: pl.BlockSpec(s, lambda i: (0, 0))
    return pl.pallas_call(
        functools.partial(finish_kernel, first_level, cross),
        grid=(rows // CHUNK,),
        in_specs=[cur(hid), cur(p0), cur(p1), cur(decay), cur(codes), fixed(scale.shape), fixed(spread.shape),
                  cur(y), fixed(carried.shape), fixed(gain.shape)],
        out_specs=cur(hid),
        out_shape=jax.ShapeDtypeStruct((rows, width), BF16),
        scratch_shapes=[pltpu.VMEM((1, width), F32)],
        name="finish",
    )(hid, p0, p1, decay, codes, scale, spread, y, carried, gain)


def from_behind(x, axis, by):
    length = lax.axis_size(axis)
    pairs = [(i, i + by) for i in range(length) if 0 <= i + by < length]
    return lax.ppermute(x, axis, pairs)


def partner(x, axis, distance):
    return lax.ppermute(x, axis, [(i, i ^ 1 << distance) for i in range(lax.axis_size(axis))])


def gather_rows(x, axis):
    pos = lax.axis_index(axis)
    for bit in range(lax.axis_size(axis).bit_length() - 1):
        other = partner(x, axis, bit)
        upper = ((pos >> bit) & 1) == 1
        x = jnp.concatenate([jnp.where(upper, other, x), jnp.where(upper, x, other)], axis=0)
    return x


def body(
    residual_in,
    query_rows,
    key_rows,
    value_rows,
    bc_weight,
    decay_rate,
    level_codes,
    level_scale,
    positions,
    ssm_gain,
):
    row_count, width = residual_in.shape
    line = ("seq", "fsdp")
    edge_k, edge_v = from_behind((key_rows[row_count - WINDOW :], value_rows[row_count - WINDOW :]), line, 1)
    hid, part = attention(
        query_rows, key_rows, value_rows, edge_k, edge_v, positions, residual_in, gather_rows(bc_weight, "fsdp")
    )
    head_bits = lax.axis_size("head").bit_length() - 1
    for bit in range(head_bits - 1):
        other = partner(part, "head", bit)
        part = (part.astype(F32) + other.astype(F32)).astype(BF16)
    other = partner(part, "head", head_bits - 1) if head_bits else jnp.zeros_like(part)
    spread = spread_matrix(decay_rate.shape[1], width)
    scale = level_scale[None, :]
    state, gone = block_state(hid, part, other, decay_rate, spread)
    y = local_terms(hid, part, other, decay_rate, level_codes, scale, spread)
    shard_pos = lax.axis_index(line)
    cross = lax.axis_size(line).bit_length() - 1
    before = jnp.ones_like(gone)
    carried = []
    for bit in range(cross):
        other_state, other_gone = partner((state.astype(BF16), gone), line, bit)
        other_state = other_state.astype(F32)
        upper = ((shard_pos >> bit) & 1) == 1
        carried.append(jnp.where(upper, other_state * before, 0.0).astype(BF16))
        state = jnp.where(upper, other_state * gone + state, state * other_gone + other_state)
        before = jnp.where(upper, before * other_gone, before)
        gone = gone * other_gone
    local_bits = row_count.bit_length() - 1
    return finish(
        local_bits + 1, cross, hid, part, other, decay_rate, level_codes, scale, spread, y,
        jnp.concatenate(carried, axis=0), ssm_gain[None, :],
    )


def solution(mesh):
    in_specs = (
        P(("groups", "seq", "fsdp"), "head"),
        P(("groups", "seq", "fsdp"), "head"),
        P(("groups", "seq", "fsdp"), "head"),
        P(("groups", "seq", "fsdp"), "head"),
        P(("head", "fsdp"), None),
        P(("groups", "seq", "fsdp"), "head"),
        P(("groups", "seq", "fsdp"), None),
        P(),
        P(("groups", "seq", "fsdp")),
        P("head"),
    )
    out_specs = P(("groups", "seq", "fsdp"), "head")
    return jax.shard_map(body, mesh=mesh, in_specs=in_specs, out_specs=out_specs, check_vma=False)
```

time: 234 us -> 97.3 us (0.42)
  matrix products: 92.7 us -> 0 us
  Pallas kernels: 0 us -> 49.3 us
  local copies, waits for them, and re-layouts: 53 us -> 6.45 us
  other arithmetic: 41 us -> 7.51 us
  blocking collectives: 33.2 us -> 0 us
  waiting for transfers between devices: 1.13 us -> 19.3 us
  starting transfers between devices: 11.4 us -> 13.8 us
    dot_general x22 -> x0, matrix products: 92.7 us -> none  [the longest x16 61.1 us: head_term(): return jnp.dot(mixing, values_head, preferred_element_type=jnp.float32)]
    pallas_call x0 -> x4, Pallas kernels: none -> 49.3 us  [the longest x1 16.2 us: finish(): pl.pallas_call(functools.partial(finish_kernel, first_level, cross), grid...]
    psum x1 -> x0, blocking collectives: 30.9 us -> none  [body(): bc_full = lax.psum(partial_value, 'head').astype(jnp.bfloat16)]
    ppermute x5 -> x7, waiting for transfers between devices: 1.13 us -> 19.3 us  [partner(): lax.ppermute(x, axis, [(i, i ^ 1 << distance) for i in range(lax.axis_siz...]
    slice x9 -> x0, local copies, waits for them, and re-layouts: 13.7 us -> none  [the longest x1 4.13 us: window_attention(): value_blocks[:block_total]]
    mul x8 -> x0, local copies, waits for them, and re-layouts: 10.8 us -> none  [the longest x2 7.98 us: body(): jnp.exp(log_end[None, :] - log_cum)[:, :, None]]
    another operation x5 -> x0, other arithmetic: 7.67 us -> none
    unnamed x3 -> x0, other arithmetic: 7.28 us -> none
  transfers between devices with their start and end apart: 7 -> 9, of which waited for: 1 -> 3; matrix products, arithmetic and copies ran while one was open for 61% -> 8% of each run, Pallas kernels for 0% -> 13%
where the time goes in v1:
time: 97.3 us; the launch traced here: 96.6 us
  Pallas kernels  49.3 us (51%)
  waiting for transfers between devices  19.3 us (20%)
  starting transfers between devices  13.8 us (14%)
  other arithmetic  7.51 us (8%)
  local copies, waits for them, and re-layouts  6.45 us (7%)
    ppermute x7, waiting for transfers between devices, partner(): lax.ppermute(x, axis, [(i, i ^ 1 << distance) for i in range(lax.axis_siz...  19.3 us
    pallas_call x1, Pallas kernels, finish(): pl.pallas_call(functools.partial(finish_kernel, first_level, cross), grid...  16.2 us
    pallas_call x1, Pallas kernels, local_terms(): pl.pallas_call(functools.partial(local_kernel, steps), grid=(n,), in_spec...  12.6 us
    pallas_call x1, Pallas kernels, attention(): pl.pallas_call(attention_kernel, grid=(n,), in_specs=[cur, prev, cur, pre...  11.8 us
    pallas_call x1, Pallas kernels, block_state(): pl.pallas_call(state_kernel, grid=(rows // CHUNK,), in_specs=[cur(hid), c...  8.68 us
    ppermute x7, starting transfers between devices, partner(): lax.ppermute(x, axis, [(i, i ^ 1 << distance) for i in range(lax.axis_siz...  7.33 us
    ppermute x2, starting transfers between devices, from_behind(): return lax.ppermute(x, axis, pairs)  6.51 us
    unnamed x12, local copies, waits for them, and re-layouts  4.52 us
  transfers between devices with their start and end apart: 9, of which 3 were waited for; matrix products, arithmetic and copies ran while one was open for 8% of the time, Pallas kernels for 13%

profile of v1, /device:TPU:0, one launch (start us, length us, event | category | flops | bytes accessed | tf_op | source)
XLA Modules:
  0.0 96.6 jit_solution(165439404025211903)
XLA Ops:
  0.0 0.5 collective-permute-start.2
  0.5 1.0 %slice.7 = bf16[128,1024]{1,0:T(8,128)(2,1)S(1)} slice(bf16[1024,1024]{1,0:T(8,128)(2,1)} %vc.1), slice={[896:1024], [0:1024]} | slice | bytes 524288 | tf_op jit(solution)/shard_map/slice | solution.py:281
  1.5 1.9 %collective-permute-start.1 = (bf16[128,1024]{1,0:T(8,128)(2,1)S(1)}, bf16[128,1024]{1,0:T(8,128)(2,1)S(1)}, u32[]{:S(2)}, u32[]{:S(2)}) collective-permute-start(bf16[128,1024]{1,0:T(8,128)(2,1)S(1)} %slice.7), channel_id=1, source_target_pairs={{0,1},{1,4},{4,5},{5,8},{8,9},{9,12},{12,13},{2,3},{3,6},{6,7},{7,... | collective-permute-start | bytes 786440 | tf_op jit(solution)/shard_map/ppermute | solution.py:251
  3.4 1.0 %slice.6 = bf16[128,1024]{1,0:T(8,128)(2,1)S(1)} slice(bf16[1024,1024]{1,0:T(8,128)(2,1)} %kc.1), slice={[896:1024], [0:1024]} | slice | bytes 524288 | tf_op jit(solution)/shard_map/slice | solution.py:281
  4.4 4.6 %collective-permute-start = (bf16[128,1024]{1,0:T(8,128)(2,1)S(1)}, bf16[128,1024]{1,0:T(8,128)(2,1)S(1)}, u32[]{:S(2)}, u32[]{:S(2)}) collective-permute-start(bf16[128,1024]{1,0:T(8,128)(2,1)S(1)} %slice.6), channel_id=1, source_target_pairs={{0,1},{1,4},{4,5},{5,8},{8,9},{9,12},{12,13},{2,3},{3,6},{6,7},{7,... | collective-permute-start | bytes 786440 | tf_op jit(solution)/shard_map/ppermute | solution.py:251
  9.0 1.8 %copy.14.decay = f32[1024,16]{1,0:T(8,128)} copy(f32[1024,16]{0,1:T(8,128)} %param.15) | data formatting | bytes 131072 | tf_op args[5]
  10.8 0.0 collective-permute-done.2
  10.8 1.0 %broadcast_select_fusion.1 = (bf16[512,256]{1,0:T(8,128)(2,1)S(1)}, bf16[512,256]{1,0:T(8,128)(2,1)S(1)}) fusion(bf16[512,256]{1,0:T(8,128)(2,1)S(1)} %collective-permute-done.2, bf16[512,256]{1,0:T(8,128)(2,1)} %param.14, pred[]{:T(512)S(6)} %eq.21), kind=kLoop, calls=%fused_computation.18 | loop fusion | flops 262144 | bytes 1048577 | tf_op jit(solution)/shard_map/jit(_where)/select_n | solution.py:263
  11.8 0.8 pad_maximum_fusion.1.w
  12.6 0.0 collective-permute-done.1.ev
  12.6 0.0 copy-start.2
  12.6 0.0 collective-permute-done.ek
  12.6 0.0 copy-start.3
  12.6 0.7 copy-done.2
  13.3 0.1 copy-done.3
  13.4 11.8 %window_attention.1 = (bf16[1024,1024]{1,0:T(8,128)(2,1)}, bf16[1024,256]{1,0:T(8,128)(2,1)}) custom-call(bf16[1024,1024]{1,0:T(8,128)(2,1)} %q.1, bf16[1024,1024]{1,0:T(8,128)(2,1)} %kc.1, bf16[1024,1024]{1,0:T(8,128)(2,1)} %kc.1, bf16[1024,1024]{1,0:T(8,128)(2,1)} %vc.1, bf16[1024,1024]{1,0:T(8,128)(2,1)} %vc.1, bf16[128,1024]{1,0:T(8,128)(2,1)} %copy-done.3, ...), custom_call_target="tpu_custom_call" | custom-call | tf_op jit(solution)/shard_map/window_attention/pallas_call | solution.py:70
  25.2 1.5 %collective-permute-start.3 = (bf16[1024,256]{1,0:T(8,128)(2,1)}, bf16[1024,256]{1,0:T(8,128)(2,1)S(1)}, u32[]{:S(2)}, u32[]{:S(2)}) collective-permute-start(bf16[1024,256]{1,0:T(8,128)(2,1)} %get-tuple-element.10.p0), channel_id=1, source_target_pairs={{0,2},{2,0},{1,3},{3,1},{4,6},{6,4},{5,7},{7,5},{8,10},{10,8},{9,1... | collective-permute-start | bytes 1572872 | tf_op jit(solution)/shard_map/ppermute | solution.py:255
  26.8 0.7 select_convert_fusion.1.spread
  27.5 12.3 %collective-permute-done.3.p1 = bf16[1024,256]{1,0:T(8,128)(2,1)S(1)} collective-permute-done((bf16[1024,256]{1,0:T(8,128)(2,1)}, bf16[1024,256]{1,0:T(8,128)(2,1)S(1)}, u32[]{:S(2)}, u32[]{:S(2)}) %collective-permute-start.3) | collective-permute-done | bytes 524320 | tf_op jit(solution)/shard_map/ppermute | solution.py:255
  39.8 0.0 copy-start.1
  39.8 0.8 copy-done.1
  40.7 8.7 %block_state.1 = (f32[128,1024]{1,0:T(8,128)}, f32[1,1024]{1,0:T(1,128)}) custom-call(bf16[1024,1024]{1,0:T(8,128)(2,1)} %get-tuple-element.9.hid, bf16[1024,256]{1,0:T(8,128)(2,1)} %get-tuple-element.10.p0, bf16[1024,256]{1,0:T(8,128)(2,1)} %copy-done.1, f32[1024,16]{1,0:T(8,128)} %copy.14.decay, bf16[32,1024]{1,0:T(8,128)(2,1)} %select_convert_fusion.1.spread), custom_call_target="tpu_custom_call" | custom-call | tf_op jit(solution)/shard_map/block_state/pallas_call | solution.py:121
  49.3 0.0 copy-start
  49.3 0.0 copy-start.4
  49.3 1.1 %convert_element_type.35 = bf16[128,1024]{1,0:T(8,128)(2,1)S(1)} convert(f32[128,1024]{1,0:T(8,128)} %get-tuple-element.11) | non-fusion elementwise | flops 131072 | bytes 786432 | tf_op jit(solution)/shard_map/convert_element_type | solution.py:299
  50.5 0.1 collective-permute-start.4
  50.6 0.5 collective-permute-start.5
  51.1 1.0 %collective-permute-done.5 = f32[1,1024]{1,0:T(1,128)S(1)} collective-permute-done((f32[1,1024]{1,0:T(1,128)}, f32[1,1024]{1,0:T(1,128)S(1)}, u32[]{:S(2)}, u32[]{:S(2)}) %collective-permute-start.5) | collective-permute-done | bytes 4128 | tf_op jit(solution)/shard_map/ppermute | solution.py:255
  52.1 0.0 collective-permute-done.4
  52.1 1.2 %fusion.8 = bf16[128,1024]{1,0:T(8,128)(2,1)S(1)} fusion(f32[128,1024]{1,0:T(8,128)} %get-tuple-element.11, f32[1024]{0:T(1024)S(1)} %bitcast.9, f32[1024]{0:T(1024)} %bitcast.11, bf16[128,1024]{1,0:T(8,128)(2,1)S(1)} %collective-permute-done.4, pred[]{:T(512)S(6)} %eq.23), kind=kLoop, calls=%fused_computation.19 | loop fusion | flops 917504 | bytes 1056769 | tf_op jit(solution)/shard_map/convert_element_type | solution.py:299
  53.3 1.6 %collective-permute-start.6 = (bf16[128,1024]{1,0:T(8,128)(2,1)S(1)}, bf16[128,1024]{1,0:T(8,128)(2,1)S(1)}, u32[]{:S(2)}, u32[]{:S(2)}) collective-permute-start(bf16[128,1024]{1,0:T(8,128)(2,1)S(1)} %fusion.8), channel_id=1, source_target_pairs={{0,4},{1,5},{4,0},{5,1},{8,12},{9,13},{12,8},{13,9},{2,6},{3,7},{6... | collective-permute-start | bytes 786440 | tf_op jit(solution)/shard_map/ppermute | solution.py:255
  54.9 0.7 mul.79
  55.6 0.4 collective-permute-start.7
  56.0 5.9 %collective-permute-done.7 = f32[1,1024]{1,0:T(1,128)S(1)} collective-permute-done((f32[1,1024]{1,0:T(1,128)S(1)}, f32[1,1024]{1,0:T(1,128)S(1)}, u32[]{:S(2)}, u32[]{:S(2)}) %collective-permute-start.7) | collective-permute-done | bytes 4128 | tf_op jit(solution)/shard_map/ppermute | solution.py:255
  62.0 0.0 collective-permute-done.6
  62.0 0.0 copy-done
  62.0 1.0 fusion
  63.0 2.7 %collective-permute-start.8 = (bf16[128,1024]{1,0:T(8,128)(2,1)S(1)}, bf16[128,1024]{1,0:T(8,128)(2,1)S(1)}, u32[]{:S(2)}, u32[]{:S(2)}) collective-permute-start(bf16[128,1024]{1,0:T(8,128)(2,1)S(1)} %get-tuple-element.18), channel_id=1, source_target_pairs={{0,8},{1,9},{4,12},{5,13},{8,0},{9,1},{12,4},{13,5},{2,10},{3,11},... | collective-permute-start | bytes 786440 | tf_op jit(solution)/shard_map/ppermute | solution.py:255
  65.6 0.0 copy-done.4
  65.6 1.1 %copy.15.codes = s32[1024,18]{1,0:T(8,128)} copy(s32[1024,18]{0,1:T(8,128)S(1)} %copy-done.4) | data formatting | bytes 147456 | tf_op args[6]
  66.7 12.6 %local_terms.1.y = f32[1024,1024]{1,0:T(8,128)} custom-call(bf16[1024,1024]{1,0:T(8,128)(2,1)} %get-tuple-element.9.hid, bf16[1024,256]{1,0:T(8,128)(2,1)} %get-tuple-element.10.p0, bf16[1024,256]{1,0:T(8,128)(2,1)} %copy-done.1, f32[1024,16]{1,0:T(8,128)} %copy.14.decay, s32[1024,18]{1,0:T(8,128)} %copy.15.codes, f32[1,18]{1,0:T(1,128)} %bitcast.19, ...), custom_call_target="tpu_custom_call" | custom-call | flops 2147483648 | bytes 8388608 | tf_op jit(solution)/shard_map/local_terms/pallas_call | solution.py:194
  79.3 0.0 collective-permute-done.8
  79.3 0.1 select_convert_fusion
  79.4 1.0 %pad_maximum_fusion.carried = bf16[384,1024]{1,0:T(8,128)(2,1)} fusion(bf16[128,1024]{1,0:T(8,128)(2,1)S(1)} %select_convert_fusion, bf16[128,1024]{1,0:T(8,128)(2,1)S(1)} %get-tuple-element.19, bf16[128,1024]{1,0:T(8,128)(2,1)S(1)} %get-tuple-element.17), kind=kLoop, calls=%fused_computation | loop fusion | flops 2359296 | bytes 1572864 | tf_op jit(solution)/shard_map/concatenate | solution.py:309
  80.3 16.2 %finish.1 = bf16[1024,1024]{1,0:T(8,128)(2,1)} custom-call(bf16[1024,1024]{1,0:T(8,128)(2,1)} %get-tuple-element.9.hid, bf16[1024,256]{1,0:T(8,128)(2,1)} %get-tuple-element.10.p0, bf16[1024,256]{1,0:T(8,128)(2,1)} %copy-done.1, f32[1024,16]{1,0:T(8,128)} %copy.14.decay, s32[1024,18]{1,0:T(8,128)} %copy.15.codes, f32[1,18]{1,0:T(1,128)} %bitcast.20, ...), custom_call_target="tpu_custom_call" | custom-call | tf_op jit(solution)/shard_map/finish/pallas_call | solution.py:236
  (5 shorter events, 0.0 us)
Async XLA Ops:
  0.0 10.8 %collective-permute-start.2 = (bf16[512,256]{1,0:T(8,128)(2,1)}, bf16[512,256]{1,0:T(8,128)(2,1)S(1)}, u32[]{:S(2)}, u32[]{:S(2)}) collective-permute-start(bf16[512,256]{1,0:T(8,128)(2,1)} %param.14), channel_id=1, source_target_pairs={{0,1},{1,0},{2,3},{3,2},{4,5},{5,4},{6,7},{7,6},{8,9},{9,8},{10,11... | collective-permute-start | bytes 786440 | tf_op jit(solution)/shard_map/ppermute | solution.py:255
  1.5 11.2 %collective-permute-start.1 = (bf16[128,1024]{1,0:T(8,128)(2,1)S(1)}, bf16[128,1024]{1,0:T(8,128)(2,1)S(1)}, u32[]{:S(2)}, u32[]{:S(2)}) collective-permute-start(bf16[128,1024]{1,0:T(8,128)(2,1)S(1)} %slice.7), channel_id=1, source_target_pairs={{0,1},{1,4},{4,5},{5,8},{8,9},{9,12},{12,13},{2,3},{3,6},{6,7},{7,... | collective-permute-start | bytes 786440 | tf_op jit(solution)/shard_map/ppermute | solution.py:251
  4.4 8.2 %collective-permute-start = (bf16[128,1024]{1,0:T(8,128)(2,1)S(1)}, bf16[128,1024]{1,0:T(8,128)(2,1)S(1)}, u32[]{:S(2)}, u32[]{:S(2)}) collective-permute-start(bf16[128,1024]{1,0:T(8,128)(2,1)S(1)} %slice.6), channel_id=1, source_target_pairs={{0,1},{1,4},{4,5},{5,8},{8,9},{9,12},{12,13},{2,3},{3,6},{6,7},{7,... | collective-permute-start | bytes 786440 | tf_op jit(solution)/shard_map/ppermute | solution.py:251
  12.6 0.7 copy-start.2
  12.6 0.8 copy-start.3
  25.2 14.6 %collective-permute-start.3 = (bf16[1024,256]{1,0:T(8,128)(2,1)}, bf16[1024,256]{1,0:T(8,128)(2,1)S(1)}, u32[]{:S(2)}, u32[]{:S(2)}) collective-permute-start(bf16[1024,256]{1,0:T(8,128)(2,1)} %get-tuple-element.10.p0), channel_id=1, source_target_pairs={{0,2},{2,0},{1,3},{3,1},{4,6},{6,4},{5,7},{7,5},{8,10},{10,8},{9,1... | collective-permute-start | bytes 1572872 | tf_op jit(solution)/shard_map/ppermute | solution.py:255
  39.8 0.8 copy-start.1
  49.3 12.7 %copy-start = (f32[128,1024]{1,0:T(8,128)S(1)}, f32[128,1024]{1,0:T(8,128)}, u32[]{:S(2)}) copy-start(f32[128,1024]{1,0:T(8,128)} %get-tuple-element.11) | copy-start | bytes 1572868
  49.3 16.3 %copy-start.4 = (s32[1024,18]{0,1:T(8,128)S(1)}, s32[1024,18]{0,1:T(8,128)}, u32[]{:S(2)}) copy-start(s32[1024,18]{0,1:T(8,128)} %param.16) | copy-start | bytes 221188
  50.5 1.6 %collective-permute-start.4 = (bf16[128,1024]{1,0:T(8,128)(2,1)S(1)}, bf16[128,1024]{1,0:T(8,128)(2,1)S(1)}, u32[]{:S(2)}, u32[]{:S(2)}) collective-permute-start(bf16[128,1024]{1,0:T(8,128)(2,1)S(1)} %convert_element_type.35), channel_id=1, source_target_pairs={{0,1},{1,0},{4,5},{5,4},{8,9},{9,8},{12,13},{13,12},{2,3},{3,2},{6... | collective-permute-start | bytes 786440 | tf_op jit(solution)/shard_map/ppermute | solution.py:255
  50.6 1.5 %collective-permute-start.5 = (f32[1,1024]{1,0:T(1,128)}, f32[1,1024]{1,0:T(1,128)S(1)}, u32[]{:S(2)}, u32[]{:S(2)}) collective-permute-start(f32[1,1024]{1,0:T(1,128)} %get-tuple-element.12), channel_id=1, source_target_pairs={{0,1},{1,0},{4,5},{5,4},{8,9},{9,8},{12,13},{13,12},{2,3},{3,2},{6... | collective-permute-start | bytes 12296 | tf_op jit(solution)/shard_map/ppermute | solution.py:255
  53.3 8.7 %collective-permute-start.6 = (bf16[128,1024]{1,0:T(8,128)(2,1)S(1)}, bf16[128,1024]{1,0:T(8,128)(2,1)S(1)}, u32[]{:S(2)}, u32[]{:S(2)}) collective-permute-start(bf16[128,1024]{1,0:T(8,128)(2,1)S(1)} %fusion.8), channel_id=1, source_target_pairs={{0,4},{1,5},{4,0},{5,1},{8,12},{9,13},{12,8},{13,9},{2,6},{3,7},{6... | collective-permute-start | bytes 786440 | tf_op jit(solution)/shard_map/ppermute | solution.py:255
  55.6 6.4 %collective-permute-start.7 = (f32[1,1024]{1,0:T(1,128)S(1)}, f32[1,1024]{1,0:T(1,128)S(1)}, u32[]{:S(2)}, u32[]{:S(2)}) collective-permute-start(f32[1,1024]{1,0:T(1,128)S(1)} %mul.79), channel_id=1, source_target_pairs={{0,4},{1,5},{4,0},{5,1},{8,12},{9,13},{12,8},{13,9},{2,6},{3,7},{6... | collective-permute-start | bytes 12296 | tf_op jit(solution)/shard_map/ppermute | solution.py:255
  63.0 16.3 %collective-permute-start.8 = (bf16[128,1024]{1,0:T(8,128)(2,1)S(1)}, bf16[128,1024]{1,0:T(8,128)(2,1)S(1)}, u32[]{:S(2)}, u32[]{:S(2)}) collective-permute-start(bf16[128,1024]{1,0:T(8,128)(2,1)S(1)} %get-tuple-element.18), channel_id=1, source_target_pairs={{0,8},{1,9},{4,12},{5,13},{8,0},{9,1},{12,4},{13,5},{2,10},{3,11},... | collective-permute-start | bytes 786440 | tf_op jit(solution)/shard_map/ppermute | solution.py:255

commit v2 on v1

v2 whole, which is shorter than its diff:
```python
import functools
import math

import jax
import jax.numpy as jnp
from jax import lax
from jax.experimental import pallas as pl
from jax.experimental.pallas import tpu as pltpu
from jax.sharding import PartitionSpec as P

HEAD_DIM = 128
HEAD_VALUES = 64
STATES = 128
WINDOW = 128
CHUNK = 128
LOG2E = math.log2(math.e)
F32 = jnp.float32
BF16 = jnp.bfloat16


def iota(shape, axis):
    return lax.broadcasted_iota(jnp.int32, shape, axis)


def dot(a, b):
    return jnp.dot(a, b, preferred_element_type=F32)


def dot_nt(a, b):
    return lax.dot_general(a, b, (((1,), (1,)), ((), ())), preferred_element_type=F32)


def dot_tn(a, b):
    return lax.dot_general(a, b, (((0,), (0,)), ((), ())), preferred_element_type=F32)


def split2(x):
    hi = x.astype(BF16)
    lo = (x - hi.astype(F32)).astype(BF16)
    return jnp.concatenate([hi, lo], axis=1)


def spread_matrix(heads, width):
    same = iota((2 * heads, width), 0) % heads == iota((2 * heads, width), 1) // HEAD_VALUES
    return jnp.where(same, 1.0, 0.0).astype(BF16)


def chunk_spec(rows, width, shift=0):
    return pl.BlockSpec((rows, width), lambda i: (i + shift, 0))


def fixed(shape):
    return pl.BlockSpec(shape, lambda i: (0,) * len(shape))


def cost(flops, moved):
    return pl.CostEstimate(flops=flops, bytes_accessed=moved, transcendentals=0)


def prepare_kernel(count, decay, codes, scale, cum_ref, exps, lam_ref, weight_ref):
    row = iota((CHUNK, CHUNK), 0)
    col = iota((CHUNK, CHUNK), 1)
    tri = jnp.where(row <= col, 1.0, 0.0)
    differ = row ^ col
    for c in range(count):
        rows = slice(c * CHUNK, (c + 1) * CHUNK)
        cum = jnp.dot(
            decay[:, rows] * LOG2E, tri, precision=lax.Precision.HIGHEST, preferred_element_type=F32
        ).T
        left = cum[CHUNK - 1 :, :] - cum
        cum_ref[rows, :] = cum
        exps[rows, :] = jnp.concatenate([split2(jnp.exp2(-left)), split2(jnp.exp2(-cum))], axis=1)
        lam = codes[rows, :].astype(F32) * scale[...]
        lam_ref[rows, :] = lam
        weight = jnp.broadcast_to(lam[:, 0:1], (CHUNK, CHUNK))
        for level in range(1, CHUNK.bit_length()):
            weight = jnp.where(differ >= 1 << level - 1, lam[:, level : level + 1], weight)
        weight_ref[rows, :] = jnp.where(col <= row, weight, 0.0)


def prepare(decay_t, codes, scale, count):
    heads, rows = decay_t.shape
    tall = count * CHUNK
    shapes = [(rows, heads), (rows, 4 * heads), codes.shape, (rows, CHUNK)]
    return pl.pallas_call(
        functools.partial(prepare_kernel, count),
        grid=(rows // tall,),
        in_specs=[pl.BlockSpec((heads, tall), lambda i: (0, i)), chunk_spec(tall, codes.shape[1]), fixed(scale.shape)],
        out_specs=[chunk_spec(tall, a[1]) for a in shapes],
        out_shape=[jax.ShapeDtypeStruct(a, BF16 if n == 1 else F32) for n, a in enumerate(shapes)],
        name="prepare",
        cost_estimate=cost(rows * 20000, 12 * rows * CHUNK),
    )(decay_t, codes, scale)


def attention_kernel(count, edged, q, kp, k, vp, v, pos, res, w, hid, part):
    width = q.shape[1]
    row = iota((CHUNK, CHUNK), 0)
    col = iota((CHUNK, CHUNK), 1)
    near = (row - col).astype(F32)
    far = near + float(WINDOW)
    scale = LOG2E / math.sqrt(HEAD_DIM)
    first = pl.program_id(0) == 0
    for c in range(count):
        rows = slice(c * CHUNK, (c + 1) * CHUNK)
        pos_col = jnp.broadcast_to(pos[c].astype(F32), (CHUNK, CHUNK)).T
        mask_cur = jnp.where((near >= 0) & (near <= pos_col), 0.0, -jnp.inf)
        mask_prev = jnp.where((far < float(WINDOW)) & (far <= pos_col), 0.0, -jnp.inf)
        mask = jnp.concatenate([mask_prev, mask_cur], axis=1)
        for h in range(width // HEAD_DIM):
            cols = slice(h * HEAD_DIM, (h + 1) * HEAD_DIM)
            if c:
                both = slice((c - 1) * CHUNK, (c + 1) * CHUNK)
                keys, vals = k[both, cols], v[both, cols]
            else:
                k_prev, v_prev = kp[:, cols], vp[:, cols]
                if edged is not None:
                    k_prev = jnp.where(first, edged[0][:CHUNK, cols], k_prev)
                    v_prev = jnp.where(first, edged[0][CHUNK:, cols], v_prev)
                keys = jnp.concatenate([k_prev, k[rows, cols]], axis=0)
                vals = jnp.concatenate([v_prev, v[rows, cols]], axis=0)
            s = dot_nt(q[rows, cols], keys) + mask
            top = jnp.max(s, axis=1, keepdims=True)
            e = jnp.exp2((s - top) * scale)
            total = jnp.sum(e, axis=1, keepdims=True)
            att = dot(e.astype(BF16), vals) * (1.0 / total)
            hid[rows, cols] = (res[rows, cols].astype(F32) + att).astype(BF16)
        part[rows, :] = dot(hid[rows, :], w[...]).astype(BF16)


def edged_kernel(count, edge, *refs):
    attention_kernel(count, (edge,), *refs)


def attention(q, k, v, edge, positions, res, w, start, stop, count):
    rows, width = q.shape
    n = rows // CHUNK
    tall = count * CHUNK
    base = start // count
    cur = chunk_spec(tall, width, base)
    prev = pl.BlockSpec((CHUNK, width), lambda i: (jnp.maximum((i + base) * count - 1, 0), 0))
    specs = [cur, prev, cur, prev, cur,
             pl.BlockSpec((count, 1, CHUNK), lambda i: (i + base, 0, 0)), cur, fixed(w.shape)]
    args = (q, k, k, v, v, positions.reshape(n, 1, CHUNK), res, w)
    kernel = functools.partial(attention_kernel, count, None)
    if edge is not None:
        specs, args = [fixed(edge.shape)] + specs, (edge,) + args
        kernel = functools.partial(edged_kernel, count)
    out_rows = (stop - start) * CHUNK
    return pl.pallas_call(
        kernel,
        grid=((stop - start) // count,),
        in_specs=specs,
        out_specs=[chunk_spec(tall, width), chunk_spec(tall, w.shape[1])],
        out_shape=[jax.ShapeDtypeStruct((out_rows, width), BF16),
                   jax.ShapeDtypeStruct((out_rows, w.shape[1]), BF16)],
        name="window_attention",
        cost_estimate=cost(out_rows * width * 4000, 10 * out_rows * width),
    )(*args)


def chunk_state(b, u, exps, spread):
    scaled = dot(exps[:, : exps.shape[1] // 2], spread) * u.astype(F32)
    return dot_tn(b, scaled.astype(BF16))


def reach_of(exps, spread):
    return dot(exps[:, exps.shape[1] // 2 :], spread)


def state_kernel(count, hid, p0, p1, exps, spread, state, gone):
    @pl.when(pl.program_id(0) == 0)
    def _():
        state[...] = jnp.zeros_like(state)
        gone[...] = jnp.ones_like(gone)

    for c in range(count):
        rows = slice(c * CHUNK, (c + 1) * CHUNK)
        b = (p0[rows, :STATES].astype(F32) + p1[rows, :STATES].astype(F32)).astype(BF16)
        d = reach_of(exps[(c + 1) * CHUNK - 16 : (c + 1) * CHUNK, :], spread[...])[15:16, :]
        state[...] = state[...] * d + chunk_state(b, hid[rows, :], exps[rows, :], spread[...])
        gone[...] = gone[...] * d


def block_state(hid, p0, p1, exps, spread, start, count):
    rows, width = hid.shape
    tall = count * CHUNK
    base = start // count
    return pl.pallas_call(
        functools.partial(state_kernel, count),
        grid=(rows // tall,),
        in_specs=[chunk_spec(tall, width), chunk_spec(tall, p0.shape[1]), chunk_spec(tall, p1.shape[1]),
                  chunk_spec(tall, exps.shape[1], base), fixed(spread.shape)],
        out_specs=[fixed((STATES, width)), fixed((1, width))],
        out_shape=[jax.ShapeDtypeStruct((STATES, width), F32), jax.ShapeDtypeStruct((1, width), F32)],
        name="block_state",
        cost_estimate=cost(rows * width * 4000, 4 * rows * width),
    )(hid, p0, p1, exps, spread)


def local_kernel(count, inner, outer, hid, p0, p1, cum_ref, exps, lam_ref, weight, spread, given, y, held):
    i = pl.program_id(0)
    width = hid.shape[1]
    low_levels = CHUNK.bit_length()
    steps = inner + outer

    @pl.when(i == 0)
    def _():
        held[...] = jnp.zeros_like(held)
        if outer:
            held[inner * STATES : steps * STATES, :] = given[...]

    left_lane = iota((CHUNK, CHUNK), 1) < HEAD_VALUES
    for c in range(count):
        rows = slice(c * CHUNK, (c + 1) * CHUNK)
        bc = (p0[rows, :].astype(F32) + p1[rows, :].astype(F32)).astype(BF16)
        b, cc = bc[:, :STATES], bc[:, STATES:]
        cum = cum_ref[rows, :]
        lam = lam_ref[rows, :]
        cum_t = cum.T
        shared = dot_nt(cc, b) * weight[rows, :]
        c32 = cc.astype(F32)
        reach = reach_of(exps[rows, :], spread[...])
        d = reach[CHUNK - 1 :, :]
        if steps:
            reads = jnp.concatenate(
                [(c32 * lam[:, low_levels + s : low_levels + s + 1]).astype(BF16) for s in range(steps)], axis=1
            )
        for g in range(width // CHUNK):
            cols = slice(g * CHUNK, (g + 1) * CHUNK)
            u = hid[rows, cols]
            zero = jnp.zeros_like(u)
            mixes = []
            for h in (2 * g, 2 * g + 1):
                gap = jnp.minimum(cum_t[h : h + 1, :] - cum[:, h : h + 1], 0.0)
                mixes.append((shared * jnp.exp2(gap)).astype(BF16))
            stack = jnp.concatenate([jnp.where(left_lane, u, zero), jnp.where(left_lane, zero, u)], axis=0)
            term = dot(jnp.concatenate(mixes, axis=1), stack)
            if steps:
                term += dot(reads, held[: steps * STATES, cols].astype(BF16)) * reach[:, cols]
            y[rows, cols] = term
        if inner:
            total = chunk_state(b, hid[rows, :], exps[rows, :], spread[...])
        after = i * count + c + 1
        for s in range(steps):
            part = slice(s * STATES, (s + 1) * STATES)
            moved = held[part, :] * d
            if s == inner:
                held[part, :] = moved
                continue
            bit = (after >> s) & 1
            fresh = jnp.where((after & ((1 << s) - 1)) == 0, 1, 0)
            held[part, :] = moved * (bit * (1 - fresh)).astype(F32) + total * (bit * fresh).astype(F32)
            total += moved


def local_terms(hid, p0, p1, prepared, spread, given, start, count):
    rows, width = hid.shape
    cum, exps, lam, weight = prepared
    tall = count * CHUNK
    base = start // count
    inner = (rows // CHUNK).bit_length() - 1
    outer = 1 if start else 0
    return pl.pallas_call(
        functools.partial(local_kernel, count, inner, outer),
        grid=(rows // tall,),
        in_specs=[chunk_spec(tall, width), chunk_spec(tall, p0.shape[1]), chunk_spec(tall, p1.shape[1])]
        + [chunk_spec(tall, a.shape[1], base) for a in (cum, exps, lam, weight)]
        + [fixed(spread.shape), fixed(given.shape)],
        out_specs=chunk_spec(tall, width),
        out_shape=jax.ShapeDtypeStruct((rows, width), F32),
        scratch_shapes=[pltpu.VMEM((max(inner + outer, 1) * STATES, width), F32)],
        name="local_terms",
        cost_estimate=cost(rows * width * 6000, 8 * rows * width),
    )(hid, p0, p1, cum, exps, lam, weight, spread, given)


def finish_kernel(count, first_level, cross, hid, p0, p1, exps, lam_ref, spread, y, carried, gain, begin, *rest):
    out, past = rest[-2:]
    width = hid.shape[1]

    @pl.when(pl.program_id(0) == 0)
    def _():
        past[...] = begin[...]

    side = (CHUNK, CHUNK)
    group = jnp.where(iota(side, 0) // HEAD_VALUES == iota(side, 1) // HEAD_VALUES, 1.0 / HEAD_VALUES, 0.0).astype(BF16)
    for n in range(count):
        rows = slice(n * CHUNK, (n + 1) * CHUNK)
        lam = lam_ref[rows, :]
        reach = reach_of(exps[rows, :], spread[...])
        c = (p0[rows, STATES:].astype(F32) + p1[rows, STATES:].astype(F32)).astype(BF16).astype(F32)
        reads = jnp.concatenate(
            [(c * lam[:, first_level + s : first_level + s + 1]).astype(BF16) for s in range(cross)], axis=1
        )
        for g in range(width // CHUNK):
            cols = slice(g * CHUNK, (g + 1) * CHUNK)
            term = y[rows, cols] + dot(reads, carried[:, cols]) * (reach[:, cols] * past[:, cols])
            mean = dot((term * term).astype(BF16), group)
            out[rows, cols] = (
                hid[rows, cols].astype(F32) + term * lax.rsqrt(mean + 1e-05) * gain[:, cols]
            ).astype(BF16)
        past[...] = past[...] * reach[CHUNK - 1 :, :]


def finish(first_level, cross, hid, p0, p1, prepared, spread, y, carried, gain, begin, whole, start, count, row_count):
    rows, width = hid.shape
    cum, exps, lam, weight = prepared
    tall = count * CHUNK
    base = start // count
    specs = [chunk_spec(tall, width), chunk_spec(tall, p0.shape[1]), chunk_spec(tall, p1.shape[1]),
             chunk_spec(tall, exps.shape[1], base), chunk_spec(tall, lam.shape[1], base), fixed(spread.shape),
             chunk_spec(tall, width), fixed(carried.shape), fixed(gain.shape), fixed(begin.shape)]
    args = (hid, p0, p1, exps, lam, spread, y, carried, gain, begin)
    aliases = {}
    if whole is not None:
        aliases = {len(specs): 0}
        specs, args = specs + [pl.BlockSpec(memory_space=pl.ANY)], args + (whole,)
    return pl.pallas_call(
        functools.partial(finish_kernel, count, first_level, cross),
        grid=(rows // tall,),
        in_specs=specs,
        out_specs=chunk_spec(tall, width, base),
        out_shape=jax.ShapeDtypeStruct((row_count, width), BF16),
        scratch_shapes=[pltpu.VMEM((1, width), F32)],
        input_output_aliases=aliases,
        name="finish",
    )(*args)


def from_behind(x, axis, by):
    length = lax.axis_size(axis)
    pairs = [(i, i + by) for i in range(length) if 0 <= i + by < length]
    return lax.ppermute(x, axis, pairs)


def partner(x, axis, distance):
    return lax.ppermute(x, axis, [(i, i ^ 1 << distance) for i in range(lax.axis_size(axis))])


def gather_rows(x, axis):
    pos = lax.axis_index(axis)
    for bit in range(lax.axis_size(axis).bit_length() - 1):
        other = partner(x, axis, bit)
        upper = ((pos >> bit) & 1) == 1
        x = jnp.concatenate([jnp.where(upper, other, x), jnp.where(upper, x, other)], axis=0)
    return x


def body(
    residual_in,
    query_rows,
    key_rows,
    value_rows,
    bc_weight,
    decay_rate,
    level_codes,
    level_scale,
    positions,
    ssm_gain,
):
    row_count, width = residual_in.shape
    line = ("seq", "fsdp")
    chunks = row_count // CHUNK
    half = chunks // 2
    count = 2
    edge = from_behind(
        jnp.concatenate([key_rows[row_count - WINDOW :], value_rows[row_count - WINDOW :]], axis=0), line, 1
    )
    weight = gather_rows(bc_weight, "fsdp")
    spread = spread_matrix(decay_rate.shape[1], width)
    prepared = prepare(decay_rate.T, level_codes, level_scale[None, :], count)
    exps = prepared[1]
    head_bits = lax.axis_size("head").bit_length() - 1

    def exchange(part):
        for bit in range(head_bits - 1):
            other = partner(part, "head", bit)
            part = (part.astype(F32) + other.astype(F32)).astype(BF16)
        other = partner(part, "head", head_bits - 1) if head_bits else jnp.zeros_like(part)
        return part, other

    inputs = (query_rows, key_rows, value_rows)
    hid_b, part_b = attention(*inputs, None, positions, residual_in, weight, half, chunks, count)
    pair_b = exchange(part_b)
    hid_a, part_a = attention(*inputs, edge, positions, residual_in, weight, 0, half, count)
    pair_a = exchange(part_a)
    state_b, gone_b = block_state(hid_b, *pair_b, exps, spread, half, count)
    state_a, gone_a = block_state(hid_a, *pair_a, exps, spread, 0, count)
    y_b = local_terms(hid_b, *pair_b, prepared, spread, state_a, half, count)
    y_a = local_terms(hid_a, *pair_a, prepared, spread, state_a, 0, count)
    state = state_a * gone_b + state_b
    gone = gone_a * gone_b
    shard_pos = lax.axis_index(line)
    cross = lax.axis_size(line).bit_length() - 1
    before = jnp.ones_like(gone)
    carried = []
    for bit in range(cross):
        other_state, other_gone = partner((state.astype(BF16), gone), line, bit)
        other_state = other_state.astype(F32)
        upper = ((shard_pos >> bit) & 1) == 1
        carried.append(jnp.where(upper, other_state * before, 0.0).astype(BF16))
        state = jnp.where(upper, other_state * gone + state, state * other_gone + other_state)
        before = jnp.where(upper, before * other_gone, before)
        gone = gone * other_gone
    carried = jnp.concatenate(carried, axis=0)
    level = row_count.bit_length()
    gain = ssm_gain[None, :]
    ones = jnp.ones_like(gone)
    out = finish(level, cross, hid_a, *pair_a, prepared, spread, y_a, carried, gain, ones, None, 0, count, row_count)
    return finish(
        level, cross, hid_b, *pair_b, prepared, spread, y_b, carried, gain, gone_a, out, half, count, row_count
    )


def solution(mesh):
    in_specs = (
        P(("groups", "seq", "fsdp"), "head"),
        P(("groups", "seq", "fsdp"), "head"),
        P(("groups", "seq", "fsdp"), "head"),
        P(("groups", "seq", "fsdp"), "head"),
        P(("head", "fsdp"), None),
        P(("groups", "seq", "fsdp"), "head"),
        P(("groups", "seq", "fsdp"), None),
        P(),
        P(("groups", "seq", "fsdp")),
        P("head"),
    )
    out_specs = P(("groups", "seq", "fsdp"), "head")
    return jax.shard_map(body, mesh=mesh, in_specs=in_specs, out_specs=out_specs, check_vma=False)
```

time: 97.3 us -> 82.8 us (0.85)
  waiting for transfers between devices: 19.3 us -> 7.81 us
  Pallas kernels: 49.3 us -> 52.3 us
  other arithmetic: 7.51 us -> 4.87 us
  starting transfers between devices: 13.8 us -> 11.5 us
    ppermute x7 -> x8, waiting for transfers between devices: 19.3 us -> 7.81 us  [partner(): lax.ppermute(x, axis, [(i, i ^ 1 << distance) for i in range(lax.axis_siz...]
    ppermute x2 -> x1, starting transfers between devices: 6.51 us -> 1.99 us  [from_behind(): return lax.ppermute(x, axis, pairs)]
    pallas_call x4 -> x9, Pallas kernels: 49.3 us -> 52.3 us  [the longest x2 16 us: finish(): pl.pallas_call(functools.partial(finish_kernel, count, first_level, cross...]
    ppermute x7 -> x8, starting transfers between devices: 7.33 us -> 9.52 us  [partner(): lax.ppermute(x, axis, [(i, i ^ 1 << distance) for i in range(lax.axis_siz...]
    unnamed x12 -> x15, local copies, waits for them, and re-layouts: 4.52 us -> 3.23 us
    convert_element_type x2, other arithmetic: 2.3 us -> 1.24 us  [body(): other_state, other_gone = partner((state.astype(BF16), gone), line, bit)]
  transfers between devices with their start and end apart: 9 -> 9, of which waited for: 3 -> 3; matrix products, arithmetic and copies ran while one was open for 8% -> 7% of each run, Pallas kernels for 13% -> 40%
where the time goes in v2:
time: 82.8 us; the launch traced here: 82.4 us
  Pallas kernels  52.3 us (63%)
  starting transfers between devices  11.5 us (14%)
  waiting for transfers between devices  7.81 us (9%)
  local copies, waits for them, and re-layouts  5.76 us (7%)
  other arithmetic  4.87 us (6%)
    pallas_call x2, Pallas kernels, finish(): pl.pallas_call(functools.partial(finish_kernel, count, first_level, cross...  16 us
    pallas_call x2, Pallas kernels, attention(): pl.pallas_call(kernel, grid=((stop - start) // count,), in_specs=specs, o...  12.7 us
    pallas_call x2, Pallas kernels, local_terms(): pl.pallas_call(functools.partial(local_kernel, count, inner, outer), grid...  12.2 us
    ppermute x8, starting transfers between devices, partner(): lax.ppermute(x, axis, [(i, i ^ 1 << distance) for i in range(lax.axis_siz...  9.52 us
    ppermute x8, waiting for transfers between devices, partner(): lax.ppermute(x, axis, [(i, i ^ 1 << distance) for i in range(lax.axis_siz...  7.81 us
    pallas_call x2, Pallas kernels, block_state(): pl.pallas_call(functools.partial(state_kernel, count), grid=(rows // tall...  7.07 us
    pallas_call x1, Pallas kernels, prepare(): pl.pallas_call(functools.partial(prepare_kernel, count), grid=(rows // ta...  4.4 us
    unnamed x15, local copies, waits for them, and re-layouts  3.23 us
  transfers between devices with their start and end apart: 9, of which 3 were waited for; matrix products, arithmetic and copies ran while one was open for 7% of the time, Pallas kernels for 40%

profile of v2, /device:TPU:0, one launch (start us, length us, event | category | flops | bytes accessed | tf_op | source)
XLA Modules:
  0.0 82.4 jit_solution(9492415183797503028)
XLA Ops:
  0.0 0.5 collective-permute-start
  0.5 1.0 %slice.6 = bf16[128,1024]{1,0:T(8,128)(2,1)S(1)} slice(bf16[1024,1024]{1,0:T(8,128)(2,1)} %refs_2_.1), slice={[896:1024], [0:1024]} | slice | bytes 524288 | tf_op jit(solution)/shard_map/slice | solution.py:368
  1.5 1.0 %slice.7 = bf16[128,1024]{1,0:T(8,128)(2,1)S(1)} slice(bf16[1024,1024]{1,0:T(8,128)(2,1)} %refs_4_.1), slice={[896:1024], [0:1024]} | slice | bytes 524288 | tf_op jit(solution)/shard_map/slice | solution.py:368
  2.5 2.0 %collective-permute-start.2 = (bf16[256,1024]{1,0:T(8,128)(2,1)S(1)}, bf16[256,1024]{1,0:T(8,128)(2,1)S(1)}, u32[]{:S(2)}, u32[]{:S(2)}) collective-permute-start(bf16[256,1024]{1,0:T(8,128)(2,1)S(1)} %pad_maximum_fusion.2), channel_id=1, source_target_pairs={{0,1},{1,4},{4,5},{5,8},{8,9},{9,12},{12,13},{2,3},{3,6},{6,7},{7,... | collective-permute-start | bytes 1572872 | tf_op jit(solution)/shard_map/ppermute | solution.py:334
  4.5 0.0 collective-permute-done
  4.5 0.0 copy-done.4
  4.6 0.8 %pad_maximum_fusion.1.w.refs_7_ = bf16[1024,256]{1,0:T(8,128)(2,1)} fusion(bf16[512,256]{1,0:T(8,128)(2,1)S(1)} %get-tuple-element.34, bf16[512,256]{1,0:T(8,128)(2,1)S(1)} %get-tuple-element.33), kind=kLoop, calls=%fused_computation.15 | loop fusion | flops 1048576 | bytes 1048576 | tf_op jit(solution)/shard_map/concatenate | solution.py:346
  5.4 6.2 %window_attention.2 = (bf16[512,1024]{1,0:T(8,128)(2,1)}, bf16[512,256]{1,0:T(8,128)(2,1)}) custom-call(bf16[1024,1024]{1,0:T(8,128)(2,1)} %refs_0_.1, bf16[1024,1024]{1,0:T(8,128)(2,1)} %refs_2_.1, bf16[1024,1024]{1,0:T(8,128)(2,1)} %refs_2_.1, bf16[1024,1024]{1,0:T(8,128)(2,1)} %refs_4_.1, bf16[1024,1024]{1,0:T(8,128)(2,1)} %refs_4_.1, ...), custom_call_target="tpu_custom_call" | custom-call | flops 2097152000 | bytes 5242880 | tf_op jit(solution)/shard_map/window_attention/pallas_call | solution.py:150
  11.6 3.0 %collective-permute-start.1 = (bf16[512,256]{1,0:T(8,128)(2,1)}, bf16[512,256]{1,0:T(8,128)(2,1)S(1)}, u32[]{:S(2)}, u32[]{:S(2)}) collective-permute-start(bf16[512,256]{1,0:T(8,128)(2,1)} %get-tuple-element.18.p0), channel_id=1, source_target_pairs={{0,2},{2,0},{1,3},{3,1},{4,6},{6,4},{5,7},{7,5},{8,10},{10,8},{9,1... | collective-permute-start | bytes 786440 | tf_op jit(solution)/shard_map/ppermute | solution.py:338
  14.6 0.0 collective-permute-done.2.edge
  14.6 0.8 copy-done
  15.4 6.5 %window_attention.3 = (bf16[512,1024]{1,0:T(8,128)(2,1)}, bf16[512,256]{1,0:T(8,128)(2,1)}) custom-call(bf16[256,1024]{1,0:T(8,128)(2,1)} %copy-done, bf16[1024,1024]{1,0:T(8,128)(2,1)} %refs_0_.1, bf16[1024,1024]{1,0:T(8,128)(2,1)} %refs_2_.1, bf16[1024,1024]{1,0:T(8,128)(2,1)} %refs_2_.1, bf16[1024,1024]{1,0:T(8,128)(2,1)} %refs_4_.1, ...), custom_call_target="tpu_custom_call" | custom-call | flops 2097152000 | bytes 5242880 | tf_op jit(solution)/shard_map/window_attention/pallas_call | solution.py:150
  21.9 0.1 collective-permute-start.3
  22.0 0.7 select_convert_fusion.1.spread
  22.7 0.0 copy-done.5
  22.7 1.0 %copy.12.codes = s32[1024,18]{1,0:T(8,128)} copy(s32[1024,18]{0,1:T(8,128)S(1)} %copy-done.5) | data formatting | bytes 147456 | tf_op args[6]
  23.7 4.4 %prepare.1 = (f32[1024,16]{1,0:T(8,128)}, bf16[1024,64]{1,0:T(8,128)(2,1)}, f32[1024,18]{1,0:T(8,128)}, f32[1024,128]{1,0:T(8,128)}) custom-call(f32[16,1024]{1,0:T(8,128)} %bitcast.15, s32[1024,18]{1,0:T(8,128)} %copy.12.codes, f32[1,18]{1,0:T(1,128)} %bitcast.25), custom_call_target="tpu_custom_call" | custom-call | flops 20480000 | bytes 1572864 | tf_op jit(solution)/shard_map/prepare/pallas_call | solution.py:85
  28.1 0.0 collective-permute-done.1.p1
  28.1 0.0 copy-start.2
  28.1 0.7 copy-done.2
  28.8 3.6 %block_state.3 = (f32[128,1024]{1,0:T(8,128)}, f32[1,1024]{1,0:T(1,128)}) custom-call(bf16[512,1024]{1,0:T(8,128)(2,1)} %get-tuple-element.17.hid, bf16[512,256]{1,0:T(8,128)(2,1)} %get-tuple-element.18.p0, bf16[512,256]{1,0:T(8,128)(2,1)} %copy-done.2, bf16[1024,64]{1,0:T(8,128)(2,1)} %get-tuple-element.19.exps, bf16[32,1024]{1,0:T(8,128)(2,1)} %select_convert_fusion.1.spread), custom_call_target="tpu_custom_call" | custom-call | flops 2097152000 | bytes 2097152 | tf_op jit(solution)/shard_map/block_state/pallas_call | solution.py:189
  32.4 0.0 collective-permute-done.3.p1
  32.4 0.0 copy-start.3
  32.4 0.7 copy-done.3
  33.1 3.5 %block_state.2 = (f32[128,1024]{1,0:T(8,128)}, f32[1,1024]{1,0:T(1,128)}) custom-call(bf16[512,1024]{1,0:T(8,128)(2,1)} %get-tuple-element.23.hid, bf16[512,256]{1,0:T(8,128)(2,1)} %get-tuple-element.24.p0, bf16[512,256]{1,0:T(8,128)(2,1)} %copy-done.3, bf16[1024,64]{1,0:T(8,128)(2,1)} %get-tuple-element.19.exps, bf16[32,1024]{1,0:T(8,128)(2,1)} %select_convert_fusion.1.spread), custom_call_target="tpu_custom_call" | custom-call | flops 2097152000 | bytes 2097152 | tf_op jit(solution)/shard_map/block_state/pallas_call | solution.py:189
  36.6 0.0 copy-done.1
  36.6 0.0 copy-done.6
  36.6 1.1 %fusion.12 = (bf16[128,1024]{1,0:T(8,128)(2,1)S(1)}, f32[128,1024]{1,0:T(8,128)S(1)}) fusion(f32[128,1024]{1,0:T(8,128)S(1)} %copy-done.1, f32[128,1024]{1,0:T(8,128)} %get-tuple-element.25.given, f32[1024]{0:T(1024)S(1)} %bitcast.24), kind=kLoop, calls=%fused_computation.36 | loop fusion | flops 393216 | bytes 1839104 | tf_op jit(solution)/shard_map/convert_element_type | solution.py:399
  37.7 1.2 %collective-permute-start.4 = (bf16[128,1024]{1,0:T(8,128)(2,1)S(1)}, bf16[128,1024]{1,0:T(8,128)(2,1)S(1)}, u32[]{:S(2)}, u32[]{:S(2)}) collective-permute-start(bf16[128,1024]{1,0:T(8,128)(2,1)S(1)} %get-tuple-element.31), channel_id=1, source_target_pairs={{0,1},{1,0},{4,5},{5,4},{8,9},{9,8},{12,13},{13,12},{2,3},{3,2},{6... | collective-permute-start | bytes 786440 | tf_op jit(solution)/shard_map/ppermute | solution.py:338
  39.0 0.7 mul.86
  39.6 0.0 collective-permute-start.5
  39.7 1.2 %collective-permute-done.5 = f32[1,1024]{1,0:T(1,128)S(1)} collective-permute-done((f32[1,1024]{1,0:T(1,128)S(1)}, f32[1,1024]{1,0:T(1,128)S(1)}, u32[]{:S(2)}, u32[]{:S(2)}) %collective-permute-start.5) | collective-permute-done | bytes 4128 | tf_op jit(solution)/shard_map/ppermute | solution.py:338
  40.8 1.6 %collective-permute-start.7 = (f32[1,1024]{1,0:T(1,128)S(1)}, f32[1,1024]{1,0:T(1,128)S(1)}, u32[]{:S(2)}, u32[]{:S(2)}) collective-permute-start(f32[1,1024]{1,0:T(1,128)S(1)} %mul.96), channel_id=1, source_target_pairs={{0,4},{1,5},{4,0},{5,1},{8,12},{9,13},{12,8},{13,9},{2,6},{3,7},{6... | collective-permute-start | bytes 12296 | tf_op jit(solution)/shard_map/ppermute | solution.py:338
  42.4 0.0 collective-permute-done.4
  42.4 0.1 fusion.8
  42.5 0.5 collective-permute-start.6
  43.0 5.8 %local_terms.3.y = f32[512,1024]{1,0:T(8,128)} custom-call(bf16[512,1024]{1,0:T(8,128)(2,1)} %get-tuple-element.23.hid, bf16[512,256]{1,0:T(8,128)(2,1)} %get-tuple-element.24.p0, bf16[512,256]{1,0:T(8,128)(2,1)} %copy-done.3, f32[1024,16]{1,0:T(8,128)} %get-tuple-element.21.cum_ref, bf16[1024,64]{1,0:T(8,128)(2,1)} %get-tuple-element.19.exps, ...), custom_call_target="tpu_custom_call" | custom-call | flops 3145728000 | bytes 4194304 | tf_op jit(solution)/shard_map/local_terms/pallas_call | solution.py:264
  48.9 0.0 collective-permute-done.7
  48.9 1.8 %collective-permute-done.6 = bf16[128,1024]{1,0:T(8,128)(2,1)S(1)} collective-permute-done((bf16[128,1024]{1,0:T(8,128)(2,1)S(1)}, bf16[128,1024]{1,0:T(8,128)(2,1)S(1)}, u32[]{:S(2)}, u32[]{:S(2)}) %collective-permute-start.6) | collective-permute-done | bytes 262176 | tf_op jit(solution)/shard_map/ppermute | solution.py:338
  50.7 0.3 fusion
  51.0 2.6 %collective-permute-start.8 = (bf16[128,1024]{1,0:T(8,128)(2,1)S(1)}, bf16[128,1024]{1,0:T(8,128)(2,1)S(1)}, u32[]{:S(2)}, u32[]{:S(2)}) collective-permute-start(bf16[128,1024]{1,0:T(8,128)(2,1)S(1)} %get-tuple-element.36), channel_id=1, source_target_pairs={{0,8},{1,9},{4,12},{5,13},{8,0},{9,1},{12,4},{13,5},{2,10},{3,11},... | collective-permute-start | bytes 786440 | tf_op jit(solution)/shard_map/ppermute | solution.py:338
  53.7 6.3 %local_terms.2.y = f32[512,1024]{1,0:T(8,128)} custom-call(bf16[512,1024]{1,0:T(8,128)(2,1)} %get-tuple-element.17.hid, bf16[512,256]{1,0:T(8,128)(2,1)} %get-tuple-element.18.p0, bf16[512,256]{1,0:T(8,128)(2,1)} %copy-done.2, f32[1024,16]{1,0:T(8,128)} %get-tuple-element.21.cum_ref, bf16[1024,64]{1,0:T(8,128)(2,1)} %get-tuple-element.19.exps, ...), custom_call_target="tpu_custom_call" | custom-call | flops 3145728000 | bytes 4194304 | tf_op jit(solution)/shard_map/local_terms/pallas_call | solution.py:264
  60.0 4.8 %collective-permute-done.8 = bf16[128,1024]{1,0:T(8,128)(2,1)S(1)} collective-permute-done((bf16[128,1024]{1,0:T(8,128)(2,1)S(1)}, bf16[128,1024]{1,0:T(8,128)(2,1)S(1)}, u32[]{:S(2)}, u32[]{:S(2)}) %collective-permute-start.8) | collective-permute-done | bytes 262176 | tf_op jit(solution)/shard_map/ppermute | solution.py:338
  64.8 0.1 select_convert_fusion
  64.9 0.9 %pad_maximum_fusion.carried = bf16[384,1024]{1,0:T(8,128)(2,1)} fusion(bf16[128,1024]{1,0:T(8,128)(2,1)S(1)} %select_convert_fusion, bf16[128,1024]{1,0:T(8,128)(2,1)S(1)} %get-tuple-element.37, bf16[128,1024]{1,0:T(8,128)(2,1)S(1)} %get-tuple-element.35), kind=kLoop, calls=%fused_computation | loop fusion | flops 2359296 | bytes 1572864 | tf_op jit(solution)/shard_map/concatenate | solution.py:406
  65.8 0.6 broadcast_3_begin.2.begin
  66.4 8.0 %finish.2.rest_0_ = bf16[1024,1024]{1,0:T(8,128)(2,1)} custom-call(bf16[512,1024]{1,0:T(8,128)(2,1)} %get-tuple-element.23.hid, bf16[512,256]{1,0:T(8,128)(2,1)} %get-tuple-element.24.p0, bf16[512,256]{1,0:T(8,128)(2,1)} %copy-done.3, bf16[1024,64]{1,0:T(8,128)(2,1)} %get-tuple-element.19.exps, f32[1024,18]{1,0:T(8,128)} %get-tuple-element.20.lam_ref, ...), custom_call_target="tpu_custom_call" | custom-call | tf_op jit(solution)/shard_map/finish/pallas_call | solution.py:319
  74.4 8.0 %finish.3 = bf16[1024,1024]{1,0:T(8,128)(2,1)} custom-call(bf16[512,1024]{1,0:T(8,128)(2,1)} %get-tuple-element.17.hid, bf16[512,256]{1,0:T(8,128)(2,1)} %get-tuple-element.18.p0, bf16[512,256]{1,0:T(8,128)(2,1)} %copy-done.2, bf16[1024,64]{1,0:T(8,128)(2,1)} %get-tuple-element.19.exps, ...), custom_call_target="tpu_custom_call", output_to_operand_aliasing={{}: (10, {})} | custom-call | tf_op jit(solution)/shard_map/finish/pallas_call | solution.py:319
  (13 shorter events, 0.1 us)
Async XLA Ops:
  0.0 4.5 %copy-start.4 = (bf16[512,256]{1,0:T(8,128)(2,1)S(1)}, bf16[512,256]{1,0:T(8,128)(2,1)}, u32[]{:S(2)}) copy-start(bf16[512,256]{1,0:T(8,128)(2,1)} %param.14) | copy-start | bytes 786436
  0.0 4.5 %collective-permute-start = (bf16[512,256]{1,0:T(8,128)(2,1)}, bf16[512,256]{1,0:T(8,128)(2,1)S(1)}, u32[]{:S(2)}, u32[]{:S(2)}) collective-permute-start(bf16[512,256]{1,0:T(8,128)(2,1)} %param.14), channel_id=1, source_target_pairs={{0,1},{1,0},{2,3},{3,2},{4,5},{5,4},{6,7},{7,6},{8,9},{9,8},{10,11... | collective-permute-start | bytes 786440 | tf_op jit(solution)/shard_map/ppermute | solution.py:338
  2.5 12.1 %collective-permute-start.2 = (bf16[256,1024]{1,0:T(8,128)(2,1)S(1)}, bf16[256,1024]{1,0:T(8,128)(2,1)S(1)}, u32[]{:S(2)}, u32[]{:S(2)}) collective-permute-start(bf16[256,1024]{1,0:T(8,128)(2,1)S(1)} %pad_maximum_fusion.2), channel_id=1, source_target_pairs={{0,1},{1,4},{4,5},{5,8},{8,9},{9,12},{12,13},{2,3},{3,6},{6,7},{7,... | collective-permute-start | bytes 1572872 | tf_op jit(solution)/shard_map/ppermute | solution.py:334
  11.6 11.0 %copy-start.5 = (s32[1024,18]{0,1:T(8,128)S(1)}, s32[1024,18]{0,1:T(8,128)}, u32[]{:S(2)}) copy-start(s32[1024,18]{0,1:T(8,128)} %param.16) | copy-start | bytes 221188
  11.6 16.5 %collective-permute-start.1 = (bf16[512,256]{1,0:T(8,128)(2,1)}, bf16[512,256]{1,0:T(8,128)(2,1)S(1)}, u32[]{:S(2)}, u32[]{:S(2)}) collective-permute-start(bf16[512,256]{1,0:T(8,128)(2,1)} %get-tuple-element.18.p0), channel_id=1, source_target_pairs={{0,2},{2,0},{1,3},{3,1},{4,6},{6,4},{5,7},{7,5},{8,10},{10,8},{9,1... | collective-permute-start | bytes 786440 | tf_op jit(solution)/shard_map/ppermute | solution.py:338
  14.6 0.8 copy-start
  21.9 10.5 %collective-permute-start.3 = (bf16[512,256]{1,0:T(8,128)(2,1)}, bf16[512,256]{1,0:T(8,128)(2,1)S(1)}, u32[]{:S(2)}, u32[]{:S(2)}) collective-permute-start(bf16[512,256]{1,0:T(8,128)(2,1)} %get-tuple-element.24.p0), channel_id=1, source_target_pairs={{0,2},{2,0},{1,3},{3,1},{4,6},{6,4},{5,7},{7,5},{8,10},{10,8},{9,1... | collective-permute-start | bytes 786440 | tf_op jit(solution)/shard_map/ppermute | solution.py:338
  28.1 0.7 copy-start.2
  32.4 0.7 copy-start.3
  33.1 3.5 %copy-start.1 = (f32[128,1024]{1,0:T(8,128)S(1)}, f32[128,1024]{1,0:T(8,128)}, u32[]{:S(2)}) copy-start(f32[128,1024]{1,0:T(8,128)} %get-tuple-element.27) | copy-start | bytes 1572868
  33.1 3.5 %copy-start.6 = (f32[1,1024]{1,0:T(1,128)S(1)}, f32[1,1024]{1,0:T(1,128)}, u32[]{:S(2)}) copy-start(f32[1,1024]{1,0:T(1,128)} %get-tuple-element.26) | copy-start | bytes 12292
  37.7 4.7 %collective-permute-start.4 = (bf16[128,1024]{1,0:T(8,128)(2,1)S(1)}, bf16[128,1024]{1,0:T(8,128)(2,1)S(1)}, u32[]{:S(2)}, u32[]{:S(2)}) collective-permute-start(bf16[128,1024]{1,0:T(8,128)(2,1)S(1)} %get-tuple-element.31), channel_id=1, source_target_pairs={{0,1},{1,0},{4,5},{5,4},{8,9},{9,8},{12,13},{13,12},{2,3},{3,2},{6... | collective-permute-start | bytes 786440 | tf_op jit(solution)/shard_map/ppermute | solution.py:338
  39.6 1.2 %collective-permute-start.5 = (f32[1,1024]{1,0:T(1,128)S(1)}, f32[1,1024]{1,0:T(1,128)S(1)}, u32[]{:S(2)}, u32[]{:S(2)}) collective-permute-start(f32[1,1024]{1,0:T(1,128)S(1)} %mul.86), channel_id=1, source_target_pairs={{0,1},{1,0},{4,5},{5,4},{8,9},{9,8},{12,13},{13,12},{2,3},{3,2},{6... | collective-permute-start | bytes 12296 | tf_op jit(solution)/shard_map/ppermute | solution.py:338
  40.8 8.1 %collective-permute-start.7 = (f32[1,1024]{1,0:T(1,128)S(1)}, f32[1,1024]{1,0:T(1,128)S(1)}, u32[]{:S(2)}, u32[]{:S(2)}) collective-permute-start(f32[1,1024]{1,0:T(1,128)S(1)} %mul.96), channel_id=1, source_target_pairs={{0,4},{1,5},{4,0},{5,1},{8,12},{9,13},{12,8},{13,9},{2,6},{3,7},{6... | collective-permute-start | bytes 12296 | tf_op jit(solution)/shard_map/ppermute | solution.py:338
  42.5 8.2 %collective-permute-start.6 = (bf16[128,1024]{1,0:T(8,128)(2,1)S(1)}, bf16[128,1024]{1,0:T(8,128)(2,1)S(1)}, u32[]{:S(2)}, u32[]{:S(2)}) collective-permute-start(bf16[128,1024]{1,0:T(8,128)(2,1)S(1)} %fusion.8), channel_id=1, source_target_pairs={{0,4},{1,5},{4,0},{5,1},{8,12},{9,13},{12,8},{13,9},{2,6},{3,7},{6... | collective-permute-start | bytes 786440 | tf_op jit(solution)/shard_map/ppermute | solution.py:338
  51.0 13.8 %collective-permute-start.8 = (bf16[128,1024]{1,0:T(8,128)(2,1)S(1)}, bf16[128,1024]{1,0:T(8,128)(2,1)S(1)}, u32[]{:S(2)}, u32[]{:S(2)}) collective-permute-start(bf16[128,1024]{1,0:T(8,128)(2,1)S(1)} %get-tuple-element.36), channel_id=1, source_target_pairs={{0,8},{1,9},{4,12},{5,13},{8,0},{9,1},{12,4},{13,5},{2,10},{3,11},... | collective-permute-start | bytes 786440 | tf_op jit(solution)/shard_map/ppermute | solution.py:338

commit v3 on v2

--- a/solution.py
+++ b/solution.py
@@ -107,25 +107,32 @@
         mask_cur = jnp.where((near >= 0) & (near <= pos_col), 0.0, -jnp.inf)
         mask_prev = jnp.where((far < float(WINDOW)) & (far <= pos_col), 0.0, -jnp.inf)
         mask = jnp.concatenate([mask_prev, mask_cur], axis=1)
-        for h in range(width // HEAD_DIM):
-            cols = slice(h * HEAD_DIM, (h + 1) * HEAD_DIM)
+        heads = [slice(h * HEAD_DIM, (h + 1) * HEAD_DIM) for h in range(width // HEAD_DIM)]
+        keys, vals = [], []
+        for cols in heads:
             if c:
                 both = slice((c - 1) * CHUNK, (c + 1) * CHUNK)
-                keys, vals = k[both, cols], v[both, cols]
+                keys.append(k[both, cols])
+                vals.append(v[both, cols])
             else:
                 k_prev, v_prev = kp[:, cols], vp[:, cols]
                 if edged is not None:
                     k_prev = jnp.where(first, edged[0][:CHUNK, cols], k_prev)
                     v_prev = jnp.where(first, edged[0][CHUNK:, cols], v_prev)
-                keys = jnp.concatenate([k_prev, k[rows, cols]], axis=0)
-                vals = jnp.concatenate([v_prev, v[rows, cols]], axis=0)
-            s = dot_nt(q[rows, cols], keys) + mask
-            top = jnp.max(s, axis=1, keepdims=True)
-            e = jnp.exp2((s - top) * scale)
-            total = jnp.sum(e, axis=1, keepdims=True)
-            att = dot(e.astype(BF16), vals) * (1.0 / total)
-            hid[rows, cols] = (res[rows, cols].astype(F32) + att).astype(BF16)
-        part[rows, :] = dot(hid[rows, :], w[...]).astype(BF16)
+                keys.append(jnp.concatenate([k_prev, k[rows, cols]], axis=0))
+                vals.append(jnp.concatenate([v_prev, v[rows, cols]], axis=0))
+        scores = [dot_nt(q[rows, cols], key) + mask for cols, key in zip(heads, keys)]
+        tops = [jnp.max(s, axis=1, keepdims=True) for s in scores]
+        raised = [jnp.exp2((s - top) * scale) for s, top in zip(scores, tops)]
+        totals = [jnp.sum(e, axis=1, keepdims=True) for e in raised]
+        sums = [dot(e.astype(BF16), val) for e, val in zip(raised, vals)]
+        tiles = [
+            (res[rows, cols].astype(F32) + att * (1.0 / total)).astype(BF16)
+            for cols, att, total in zip(heads, sums, totals)
+        ]
+        hidden = jnp.concatenate(tiles, axis=1)
+        hid[rows, :] = hidden
+        part[rows, :] = dot(hidden, w[...]).astype(BF16)
 
 
 def edged_kernel(count, edge, *refs):
@@ -226,6 +233,7 @@
             reads = jnp.concatenate(
                 [(c32 * lam[:, low_levels + s : low_levels + s + 1]).astype(BF16) for s in range(steps)], axis=1
             )
+        terms = []
         for g in range(width // CHUNK):
             cols = slice(g * CHUNK, (g + 1) * CHUNK)
             u = hid[rows, cols]
@@ -235,10 +243,11 @@
                 gap = jnp.minimum(cum_t[h : h + 1, :] - cum[:, h : h + 1], 0.0)
                 mixes.append((shared * jnp.exp2(gap)).astype(BF16))
             stack = jnp.concatenate([jnp.where(left_lane, u, zero), jnp.where(left_lane, zero, u)], axis=0)
-            term = dot(jnp.concatenate(mixes, axis=1), stack)
-            if steps:
-                term += dot(reads, held[: steps * STATES, cols].astype(BF16)) * reach[:, cols]
-            y[rows, cols] = term
+            terms.append(dot(jnp.concatenate(mixes, axis=1), stack))
+        term = jnp.concatenate(terms, axis=1)
+        if steps:
+            term += dot(reads, held[: steps * STATES, :].astype(BF16)) * reach
+        y[rows, :] = term
         if inner:
             total = chunk_state(b, hid[rows, :], exps[rows, :], spread[...])
         after = i * count + c + 1
@@ -283,24 +292,32 @@
     def _():
         past[...] = begin[...]
 
-    side = (CHUNK, CHUNK)
+    tile = min(2 * CHUNK, width)
+    side = (tile, tile)
     group = jnp.where(iota(side, 0) // HEAD_VALUES == iota(side, 1) // HEAD_VALUES, 1.0 / HEAD_VALUES, 0.0).astype(BF16)
+    lam = lam_ref[...]
+    c = (p0[:, STATES:].astype(F32) + p1[:, STATES:].astype(F32)).astype(BF16).astype(F32)
+    reads = jnp.concatenate(
+        [(c * lam[:, first_level + s : first_level + s + 1]).astype(BF16) for s in range(cross)], axis=1
+    )
+    reach = reach_of(exps[...], spread[...])
+    ahead = past[...]
+    scaled = []
     for n in range(count):
-        rows = slice(n * CHUNK, (n + 1) * CHUNK)
-        lam = lam_ref[rows, :]
-        reach = reach_of(exps[rows, :], spread[...])
-        c = (p0[rows, STATES:].astype(F32) + p1[rows, STATES:].astype(F32)).astype(BF16).astype(F32)
-        reads = jnp.concatenate(
-            [(c * lam[:, first_level + s : first_level + s + 1]).astype(BF16) for s in range(cross)], axis=1
-        )
-        for g in range(width // CHUNK):
-            cols = slice(g * CHUNK, (g + 1) * CHUNK)
-            term = y[rows, cols] + dot(reads, carried[:, cols]) * (reach[:, cols] * past[:, cols])
-            mean = dot((term * term).astype(BF16), group)
-            out[rows, cols] = (
-                hid[rows, cols].astype(F32) + term * lax.rsqrt(mean + 1e-05) * gain[:, cols]
-            ).astype(BF16)
-        past[...] = past[...] * reach[CHUNK - 1 :, :]
+        own = reach[n * CHUNK : (n + 1) * CHUNK, :]
+        scaled.append(own * ahead)
+        ahead = ahead * own[CHUNK - 1 :, :]
+    past[...] = ahead
+    scaled = jnp.concatenate(scaled, axis=0)
+    tiles = [slice(g * tile, (g + 1) * tile) for g in range(width // tile)]
+    terms = [y[:, cols] + dot(reads, carried[:, cols]) * scaled[:, cols] for cols in tiles]
+    means = [dot((term * term).astype(BF16), group) for term in terms]
+    results = [
+        (hid[:, cols].astype(F32) + term * lax.rsqrt(mean + 1e-05) * gain[:, cols]).astype(BF16)
+        for cols, term, mean in zip(tiles, terms, means)
+    ]
+    for cols, result in zip(tiles, results):
+        out[:, cols] = result
 
 
 def finish(first_level, cross, hid, p0, p1, prepared, spread, y, carried, gain, begin, whole, start, count, row_count):

time: 82.8 us -> 75.1 us (0.907)
  Pallas kernels: 52.3 us -> 43.4 us
    pallas_call x2, Pallas kernels: 16 us -> 8.93 us  [finish(): pl.pallas_call(functools.partial(finish_kernel, count, first_level, cross...]
    pallas_call x2, Pallas kernels: 12.7 us -> 10.9 us  [attention(): pl.pallas_call(kernel, grid=((stop - start) // count,), in_specs=specs, o...]
  transfers between devices with their start and end apart: 9 -> 9, of which waited for: 3 -> 3; matrix products, arithmetic and copies ran while one was open for 7% -> 7% of each run, Pallas kernels for 40% -> 41%
where the time goes in v3:
time: 75.1 us; the launch traced here: 74.7 us
  Pallas kernels  43.4 us (58%)
  starting transfers between devices  11.9 us (16%)
  waiting for transfers between devices  8.63 us (11%)
  local copies, waits for them, and re-layouts  5.76 us (8%)
  other arithmetic  4.87 us (6%)
    pallas_call x2, Pallas kernels, local_terms(): pl.pallas_call(functools.partial(local_kernel, count, inner, outer), grid...  12.1 us
    pallas_call x2, Pallas kernels, attention(): pl.pallas_call(kernel, grid=((stop - start) // count,), in_specs=specs, o...  10.9 us
    ppermute x8, starting transfers between devices, partner(): lax.ppermute(x, axis, [(i, i ^ 1 << distance) for i in range(lax.axis_siz...  9.87 us
    pallas_call x2, Pallas kernels, finish(): pl.pallas_call(functools.partial(finish_kernel, count, first_level, cross...  8.93 us
    ppermute x8, waiting for transfers between devices, partner(): lax.ppermute(x, axis, [(i, i ^ 1 << distance) for i in range(lax.axis_siz...  8.62 us
    pallas_call x2, Pallas kernels, block_state(): pl.pallas_call(functools.partial(state_kernel, count), grid=(rows // tall...  7.07 us
    pallas_call x1, Pallas kernels, prepare(): pl.pallas_call(functools.partial(prepare_kernel, count), grid=(rows // ta...  4.4 us
    unnamed x15, local copies, waits for them, and re-layouts  3.23 us
  transfers between devices with their start and end apart: 9, of which 3 were waited for; matrix products, arithmetic and copies ran while one was open for 7% of the time, Pallas kernels for 41%

profile of v3, /device:TPU:0, one launch (start us, length us, event | category | flops | bytes accessed | tf_op | source)
XLA Modules:
  0.0 74.7 jit_solution(2633054428434218904)
XLA Ops:
  0.0 0.5 collective-permute-start
  0.5 1.0 %slice.6 = bf16[128,1024]{1,0:T(8,128)(2,1)S(1)} slice(bf16[1024,1024]{1,0:T(8,128)(2,1)} %refs_2_.1), slice={[896:1024], [0:1024]} | slice | bytes 524288 | tf_op jit(solution)/shard_map/slice | solution.py:385
  1.5 1.0 %slice.7 = bf16[128,1024]{1,0:T(8,128)(2,1)S(1)} slice(bf16[1024,1024]{1,0:T(8,128)(2,1)} %refs_4_.1), slice={[896:1024], [0:1024]} | slice | bytes 524288 | tf_op jit(solution)/shard_map/slice | solution.py:385
  2.5 2.0 %collective-permute-start.2 = (bf16[256,1024]{1,0:T(8,128)(2,1)S(1)}, bf16[256,1024]{1,0:T(8,128)(2,1)S(1)}, u32[]{:S(2)}, u32[]{:S(2)}) collective-permute-start(bf16[256,1024]{1,0:T(8,128)(2,1)S(1)} %pad_maximum_fusion.2), channel_id=1, source_target_pairs={{0,1},{1,4},{4,5},{5,8},{8,9},{9,12},{12,13},{2,3},{3,6},{6,7},{7,... | collective-permute-start | bytes 1572872 | tf_op jit(solution)/shard_map/ppermute | solution.py:351
  4.5 0.0 collective-permute-done
  4.5 0.0 copy-done.4
  4.6 0.8 %pad_maximum_fusion.1.w.refs_7_ = bf16[1024,256]{1,0:T(8,128)(2,1)} fusion(bf16[512,256]{1,0:T(8,128)(2,1)S(1)} %get-tuple-element.34, bf16[512,256]{1,0:T(8,128)(2,1)S(1)} %get-tuple-element.33), kind=kLoop, calls=%fused_computation.15 | loop fusion | flops 1048576 | bytes 1048576 | tf_op jit(solution)/shard_map/concatenate | solution.py:363
  5.4 5.3 %window_attention.2 = (bf16[512,1024]{1,0:T(8,128)(2,1)}, bf16[512,256]{1,0:T(8,128)(2,1)}) custom-call(bf16[1024,1024]{1,0:T(8,128)(2,1)} %refs_0_.1, bf16[1024,1024]{1,0:T(8,128)(2,1)} %refs_2_.1, bf16[1024,1024]{1,0:T(8,128)(2,1)} %refs_2_.1, bf16[1024,1024]{1,0:T(8,128)(2,1)} %refs_4_.1, bf16[1024,1024]{1,0:T(8,128)(2,1)} %refs_4_.1, ...), custom_call_target="tpu_custom_call" | custom-call | flops 2097152000 | bytes 5242880 | tf_op jit(solution)/shard_map/window_attention/pallas_call | solution.py:157
  10.7 3.0 %collective-permute-start.1 = (bf16[512,256]{1,0:T(8,128)(2,1)}, bf16[512,256]{1,0:T(8,128)(2,1)S(1)}, u32[]{:S(2)}, u32[]{:S(2)}) collective-permute-start(bf16[512,256]{1,0:T(8,128)(2,1)} %get-tuple-element.18.p0), channel_id=1, source_target_pairs={{0,2},{2,0},{1,3},{3,1},{4,6},{6,4},{5,7},{7,5},{8,10},{10,8},{9,1... | collective-permute-start | bytes 786440 | tf_op jit(solution)/shard_map/ppermute | solution.py:355
  13.7 0.0 collective-permute-done.2.edge
  13.7 0.8 %copy-done = bf16[256,1024]{1,0:T(8,128)(2,1)} copy-done((bf16[256,1024]{1,0:T(8,128)(2,1)}, bf16[256,1024]{1,0:T(8,128)(2,1)S(1)}, u32[]{:S(2)}) %copy-start) | copy-done | bytes 524312
  14.5 5.6 %window_attention.3 = (bf16[512,1024]{1,0:T(8,128)(2,1)}, bf16[512,256]{1,0:T(8,128)(2,1)}) custom-call(bf16[256,1024]{1,0:T(8,128)(2,1)} %copy-done, bf16[1024,1024]{1,0:T(8,128)(2,1)} %refs_0_.1, bf16[1024,1024]{1,0:T(8,128)(2,1)} %refs_2_.1, bf16[1024,1024]{1,0:T(8,128)(2,1)} %refs_2_.1, bf16[1024,1024]{1,0:T(8,128)(2,1)} %refs_4_.1, ...), custom_call_target="tpu_custom_call" | custom-call | flops 2097152000 | bytes 5242880 | tf_op jit(solution)/shard_map/window_attention/pallas_call | solution.py:157
  20.1 0.1 collective-permute-start.3
  20.1 0.7 select_convert_fusion.1.spread
  20.9 0.0 copy-done.5
  20.9 1.0 %copy.12.codes = s32[1024,18]{1,0:T(8,128)} copy(s32[1024,18]{0,1:T(8,128)S(1)} %copy-done.5) | data formatting | bytes 147456 | tf_op args[6]
  21.9 4.4 %prepare.1 = (f32[1024,16]{1,0:T(8,128)}, bf16[1024,64]{1,0:T(8,128)(2,1)}, f32[1024,18]{1,0:T(8,128)}, f32[1024,128]{1,0:T(8,128)}) custom-call(f32[16,1024]{1,0:T(8,128)} %bitcast.15, s32[1024,18]{1,0:T(8,128)} %copy.12.codes, f32[1,18]{1,0:T(1,128)} %bitcast.25), custom_call_target="tpu_custom_call" | custom-call | flops 20480000 | bytes 1572864 | tf_op jit(solution)/shard_map/prepare/pallas_call | solution.py:85
  26.3 0.0 collective-permute-done.1.p1
  26.3 0.0 copy-start.2
  26.3 0.7 copy-done.2
  27.0 3.6 %block_state.3 = (f32[128,1024]{1,0:T(8,128)}, f32[1,1024]{1,0:T(1,128)}) custom-call(bf16[512,1024]{1,0:T(8,128)(2,1)} %get-tuple-element.17.hid, bf16[512,256]{1,0:T(8,128)(2,1)} %get-tuple-element.18.p0, bf16[512,256]{1,0:T(8,128)(2,1)} %copy-done.2, bf16[1024,64]{1,0:T(8,128)(2,1)} %get-tuple-element.19.exps, bf16[32,1024]{1,0:T(8,128)(2,1)} %select_convert_fusion.1.spread), custom_call_target="tpu_custom_call" | custom-call | flops 2097152000 | bytes 2097152 | tf_op jit(solution)/shard_map/block_state/pallas_call | solution.py:196
  30.6 0.0 collective-permute-done.3.p1
  30.6 0.0 copy-start.3
  30.6 0.7 copy-done.3
  31.3 3.5 %block_state.2 = (f32[128,1024]{1,0:T(8,128)}, f32[1,1024]{1,0:T(1,128)}) custom-call(bf16[512,1024]{1,0:T(8,128)(2,1)} %get-tuple-element.23.hid, bf16[512,256]{1,0:T(8,128)(2,1)} %get-tuple-element.24.p0, bf16[512,256]{1,0:T(8,128)(2,1)} %copy-done.3, bf16[1024,64]{1,0:T(8,128)(2,1)} %get-tuple-element.19.exps, bf16[32,1024]{1,0:T(8,128)(2,1)} %select_convert_fusion.1.spread), custom_call_target="tpu_custom_call" | custom-call | flops 2097152000 | bytes 2097152 | tf_op jit(solution)/shard_map/block_state/pallas_call | solution.py:196
  34.8 0.0 copy-done.1
  34.8 0.0 copy-done.6
  34.8 1.1 %fusion.12 = (bf16[128,1024]{1,0:T(8,128)(2,1)S(1)}, f32[128,1024]{1,0:T(8,128)S(1)}) fusion(f32[128,1024]{1,0:T(8,128)S(1)} %copy-done.1, f32[128,1024]{1,0:T(8,128)} %get-tuple-element.25.given, f32[1024]{0:T(1024)S(1)} %bitcast.24), kind=kLoop, calls=%fused_computation.36 | loop fusion | flops 393216 | bytes 1839104 | tf_op jit(solution)/shard_map/convert_element_type | solution.py:416
  35.9 1.2 %collective-permute-start.4 = (bf16[128,1024]{1,0:T(8,128)(2,1)S(1)}, bf16[128,1024]{1,0:T(8,128)(2,1)S(1)}, u32[]{:S(2)}, u32[]{:S(2)}) collective-permute-start(bf16[128,1024]{1,0:T(8,128)(2,1)S(1)} %get-tuple-element.31), channel_id=1, source_target_pairs={{0,1},{1,0},{4,5},{5,4},{8,9},{9,8},{12,13},{13,12},{2,3},{3,2},{6... | collective-permute-start | bytes 786440 | tf_op jit(solution)/shard_map/ppermute | solution.py:355
  37.1 0.7 mul.86
  37.8 0.0 collective-permute-start.5
  37.8 1.2 %collective-permute-done.5 = f32[1,1024]{1,0:T(1,128)S(1)} collective-permute-done((f32[1,1024]{1,0:T(1,128)S(1)}, f32[1,1024]{1,0:T(1,128)S(1)}, u32[]{:S(2)}, u32[]{:S(2)}) %collective-permute-start.5) | collective-permute-done | bytes 4128 | tf_op jit(solution)/shard_map/ppermute | solution.py:355
  39.0 2.4 %collective-permute-start.7 = (f32[1,1024]{1,0:T(1,128)S(1)}, f32[1,1024]{1,0:T(1,128)S(1)}, u32[]{:S(2)}, u32[]{:S(2)}) collective-permute-start(f32[1,1024]{1,0:T(1,128)S(1)} %mul.96), channel_id=1, source_target_pairs={{0,4},{1,5},{4,0},{5,1},{8,12},{9,13},{12,8},{13,9},{2,6},{3,7},{6... | collective-permute-start | bytes 12296 | tf_op jit(solution)/shard_map/ppermute | solution.py:355
  41.4 0.0 collective-permute-done.4
  41.4 0.1 fusion.8
  41.5 0.1 collective-permute-start.6
  41.6 5.9 %local_terms.3.y = f32[512,1024]{1,0:T(8,128)} custom-call(bf16[512,1024]{1,0:T(8,128)(2,1)} %get-tuple-element.23.hid, bf16[512,256]{1,0:T(8,128)(2,1)} %get-tuple-element.24.p0, bf16[512,256]{1,0:T(8,128)(2,1)} %copy-done.3, f32[1024,16]{1,0:T(8,128)} %get-tuple-element.21.cum_ref, bf16[1024,64]{1,0:T(8,128)(2,1)} %get-tuple-element.19.exps, ...), custom_call_target="tpu_custom_call" | custom-call | flops 3145728000 | bytes 4194304 | tf_op jit(solution)/shard_map/local_terms/pallas_call | solution.py:273
  47.4 0.0 collective-permute-done.7
  47.5 2.4 %collective-permute-done.6 = bf16[128,1024]{1,0:T(8,128)(2,1)S(1)} collective-permute-done((bf16[128,1024]{1,0:T(8,128)(2,1)S(1)}, bf16[128,1024]{1,0:T(8,128)(2,1)S(1)}, u32[]{:S(2)}, u32[]{:S(2)}) %collective-permute-start.6) | collective-permute-done | bytes 262176 | tf_op jit(solution)/shard_map/ppermute | solution.py:355
  49.8 0.3 fusion
  50.1 2.7 %collective-permute-start.8 = (bf16[128,1024]{1,0:T(8,128)(2,1)S(1)}, bf16[128,1024]{1,0:T(8,128)(2,1)S(1)}, u32[]{:S(2)}, u32[]{:S(2)}) collective-permute-start(bf16[128,1024]{1,0:T(8,128)(2,1)S(1)} %get-tuple-element.36), channel_id=1, source_target_pairs={{0,8},{1,9},{4,12},{5,13},{8,0},{9,1},{12,4},{13,5},{2,10},{3,11},... | collective-permute-start | bytes 786440 | tf_op jit(solution)/shard_map/ppermute | solution.py:355
  52.8 6.2 %local_terms.2.y = f32[512,1024]{1,0:T(8,128)} custom-call(bf16[512,1024]{1,0:T(8,128)(2,1)} %get-tuple-element.17.hid, bf16[512,256]{1,0:T(8,128)(2,1)} %get-tuple-element.18.p0, bf16[512,256]{1,0:T(8,128)(2,1)} %copy-done.2, f32[1024,16]{1,0:T(8,128)} %get-tuple-element.21.cum_ref, bf16[1024,64]{1,0:T(8,128)(2,1)} %get-tuple-element.19.exps, ...), custom_call_target="tpu_custom_call" | custom-call | flops 3145728000 | bytes 4194304 | tf_op jit(solution)/shard_map/local_terms/pallas_call | solution.py:273
  59.0 5.1 %collective-permute-done.8 = bf16[128,1024]{1,0:T(8,128)(2,1)S(1)} collective-permute-done((bf16[128,1024]{1,0:T(8,128)(2,1)S(1)}, bf16[128,1024]{1,0:T(8,128)(2,1)S(1)}, u32[]{:S(2)}, u32[]{:S(2)}) %collective-permute-start.8) | collective-permute-done | bytes 262176 | tf_op jit(solution)/shard_map/ppermute | solution.py:355
  64.1 0.1 select_convert_fusion
  64.2 0.9 %pad_maximum_fusion.carried = bf16[384,1024]{1,0:T(8,128)(2,1)} fusion(bf16[128,1024]{1,0:T(8,128)(2,1)S(1)} %select_convert_fusion, bf16[128,1024]{1,0:T(8,128)(2,1)S(1)} %get-tuple-element.37, bf16[128,1024]{1,0:T(8,128)(2,1)S(1)} %get-tuple-element.35), kind=kLoop, calls=%fused_computation | loop fusion | flops 2359296 | bytes 1572864 | tf_op jit(solution)/shard_map/concatenate | solution.py:423
  65.1 0.6 broadcast_3_begin.2.begin
  65.7 4.5 %finish.2.rest_0_ = bf16[1024,1024]{1,0:T(8,128)(2,1)} custom-call(bf16[512,1024]{1,0:T(8,128)(2,1)} %get-tuple-element.23.hid, bf16[512,256]{1,0:T(8,128)(2,1)} %get-tuple-element.24.p0, bf16[512,256]{1,0:T(8,128)(2,1)} %copy-done.3, bf16[1024,64]{1,0:T(8,128)(2,1)} %get-tuple-element.19.exps, f32[1024,18]{1,0:T(8,128)} %get-tuple-element.20.lam_ref, ...), custom_call_target="tpu_custom_call" | custom-call | tf_op jit(solution)/shard_map/finish/pallas_call | solution.py:336
  70.2 4.5 %finish.3 = bf16[1024,1024]{1,0:T(8,128)(2,1)} custom-call(bf16[512,1024]{1,0:T(8,128)(2,1)} %get-tuple-element.17.hid, bf16[512,256]{1,0:T(8,128)(2,1)} %get-tuple-element.18.p0, bf16[512,256]{1,0:T(8,128)(2,1)} %copy-done.2, bf16[1024,64]{1,0:T(8,128)(2,1)} %get-tuple-element.19.exps, ...), custom_call_target="tpu_custom_call", output_to_operand_aliasing={{}: (10, {})} | custom-call | tf_op jit(solution)/shard_map/finish/pallas_call | solution.py:336
  (13 shorter events, 0.1 us)
Async XLA Ops:
  0.0 4.5 %copy-start.4 = (bf16[512,256]{1,0:T(8,128)(2,1)S(1)}, bf16[512,256]{1,0:T(8,128)(2,1)}, u32[]{:S(2)}) copy-start(bf16[512,256]{1,0:T(8,128)(2,1)} %param.14) | copy-start | bytes 786436
  0.0 4.5 %collective-permute-start = (bf16[512,256]{1,0:T(8,128)(2,1)}, bf16[512,256]{1,0:T(8,128)(2,1)S(1)}, u32[]{:S(2)}, u32[]{:S(2)}) collective-permute-start(bf16[512,256]{1,0:T(8,128)(2,1)} %param.14), channel_id=1, source_target_pairs={{0,1},{1,0},{2,3},{3,2},{4,5},{5,4},{6,7},{7,6},{8,9},{9,8},{10,11... | collective-permute-start | bytes 786440 | tf_op jit(solution)/shard_map/ppermute | solution.py:355
  2.5 11.2 %collective-permute-start.2 = (bf16[256,1024]{1,0:T(8,128)(2,1)S(1)}, bf16[256,1024]{1,0:T(8,128)(2,1)S(1)}, u32[]{:S(2)}, u32[]{:S(2)}) collective-permute-start(bf16[256,1024]{1,0:T(8,128)(2,1)S(1)} %pad_maximum_fusion.2), channel_id=1, source_target_pairs={{0,1},{1,4},{4,5},{5,8},{8,9},{9,12},{12,13},{2,3},{3,6},{6,7},{7,... | collective-permute-start | bytes 1572872 | tf_op jit(solution)/shard_map/ppermute | solution.py:351
  10.7 10.1 %copy-start.5 = (s32[1024,18]{0,1:T(8,128)S(1)}, s32[1024,18]{0,1:T(8,128)}, u32[]{:S(2)}) copy-start(s32[1024,18]{0,1:T(8,128)} %param.16) | copy-start | bytes 221188
  10.7 15.6 %collective-permute-start.1 = (bf16[512,256]{1,0:T(8,128)(2,1)}, bf16[512,256]{1,0:T(8,128)(2,1)S(1)}, u32[]{:S(2)}, u32[]{:S(2)}) collective-permute-start(bf16[512,256]{1,0:T(8,128)(2,1)} %get-tuple-element.18.p0), channel_id=1, source_target_pairs={{0,2},{2,0},{1,3},{3,1},{4,6},{6,4},{5,7},{7,5},{8,10},{10,8},{9,1... | collective-permute-start | bytes 786440 | tf_op jit(solution)/shard_map/ppermute | solution.py:355
  13.7 0.8 %copy-start = (bf16[256,1024]{1,0:T(8,128)(2,1)}, bf16[256,1024]{1,0:T(8,128)(2,1)S(1)}, u32[]{:S(2)}) copy-start(bf16[256,1024]{1,0:T(8,128)(2,1)S(1)} %collective-permute-done.2.edge) | copy-start | bytes 1572868
  20.1 10.5 %collective-permute-start.3 = (bf16[512,256]{1,0:T(8,128)(2,1)}, bf16[512,256]{1,0:T(8,128)(2,1)S(1)}, u32[]{:S(2)}, u32[]{:S(2)}) collective-permute-start(bf16[512,256]{1,0:T(8,128)(2,1)} %get-tuple-element.24.p0), channel_id=1, source_target_pairs={{0,2},{2,0},{1,3},{3,1},{4,6},{6,4},{5,7},{7,5},{8,10},{10,8},{9,1... | collective-permute-start | bytes 786440 | tf_op jit(solution)/shard_map/ppermute | solution.py:355
  26.3 0.7 copy-start.2
  30.6 0.7 copy-start.3
  31.3 3.5 %copy-start.1 = (f32[128,1024]{1,0:T(8,128)S(1)}, f32[128,1024]{1,0:T(8,128)}, u32[]{:S(2)}) copy-start(f32[128,1024]{1,0:T(8,128)} %get-tuple-element.27) | copy-start | bytes 1572868
  31.3 3.5 %copy-start.6 = (f32[1,1024]{1,0:T(1,128)S(1)}, f32[1,1024]{1,0:T(1,128)}, u32[]{:S(2)}) copy-start(f32[1,1024]{1,0:T(1,128)} %get-tuple-element.26) | copy-start | bytes 12292
  35.9 5.4 %collective-permute-start.4 = (bf16[128,1024]{1,0:T(8,128)(2,1)S(1)}, bf16[128,1024]{1,0:T(8,128)(2,1)S(1)}, u32[]{:S(2)}, u32[]{:S(2)}) collective-permute-start(bf16[128,1024]{1,0:T(8,128)(2,1)S(1)} %get-tuple-element.31), channel_id=1, source_target_pairs={{0,1},{1,0},{4,5},{5,4},{8,9},{9,8},{12,13},{13,12},{2,3},{3,2},{6... | collective-permute-start | bytes 786440 | tf_op jit(solution)/shard_map/ppermute | solution.py:355
  37.8 1.2 %collective-permute-start.5 = (f32[1,1024]{1,0:T(1,128)S(1)}, f32[1,1024]{1,0:T(1,128)S(1)}, u32[]{:S(2)}, u32[]{:S(2)}) collective-permute-start(f32[1,1024]{1,0:T(1,128)S(1)} %mul.86), channel_id=1, source_target_pairs={{0,1},{1,0},{4,5},{5,4},{8,9},{9,8},{12,13},{13,12},{2,3},{3,2},{6... | collective-permute-start | bytes 12296 | tf_op jit(solution)/shard_map/ppermute | solution.py:355
  39.0 8.4 %collective-permute-start.7 = (f32[1,1024]{1,0:T(1,128)S(1)}, f32[1,1024]{1,0:T(1,128)S(1)}, u32[]{:S(2)}, u32[]{:S(2)}) collective-permute-start(f32[1,1024]{1,0:T(1,128)S(1)} %mul.96), channel_id=1, source_target_pairs={{0,4},{1,5},{4,0},{5,1},{8,12},{9,13},{12,8},{13,9},{2,6},{3,7},{6... | collective-permute-start | bytes 12296 | tf_op jit(solution)/shard_map/ppermute | solution.py:355
  41.5 8.3 %collective-permute-start.6 = (bf16[128,1024]{1,0:T(8,128)(2,1)S(1)}, bf16[128,1024]{1,0:T(8,128)(2,1)S(1)}, u32[]{:S(2)}, u32[]{:S(2)}) collective-permute-start(bf16[128,1024]{1,0:T(8,128)(2,1)S(1)} %fusion.8), channel_id=1, source_target_pairs={{0,4},{1,5},{4,0},{5,1},{8,12},{9,13},{12,8},{13,9},{2,6},{3,7},{6... | collective-permute-start | bytes 786440 | tf_op jit(solution)/shard_map/ppermute | solution.py:355
  50.1 14.0 %collective-permute-start.8 = (bf16[128,1024]{1,0:T(8,128)(2,1)S(1)}, bf16[128,1024]{1,0:T(8,128)(2,1)S(1)}, u32[]{:S(2)}, u32[]{:S(2)}) collective-permute-start(bf16[128,1024]{1,0:T(8,128)(2,1)S(1)} %get-tuple-element.36), channel_id=1, source_target_pairs={{0,8},{1,9},{4,12},{5,13},{8,0},{9,1},{12,4},{13,5},{2,10},{3,11},... | collective-permute-start | bytes 786440 | tf_op jit(solution)/shard_map/ppermute | solution.py:355

commit v4 on v3

--- a/solution.py
+++ b/solution.py
@@ -3,6 +3,7 @@
 
 import jax
 import jax.numpy as jnp
+import numpy as np
 from jax import lax
 from jax.experimental import pallas as pl
 from jax.experimental.pallas import tpu as pltpu
@@ -41,8 +42,8 @@
 
 
 def spread_matrix(heads, width):
-    same = iota((2 * heads, width), 0) % heads == iota((2 * heads, width), 1) // HEAD_VALUES
-    return jnp.where(same, 1.0, 0.0).astype(BF16)
+    same = np.arange(2 * heads)[:, None] % heads == np.arange(width)[None, :] // HEAD_VALUES
+    return jnp.asarray(same.astype(np.float32), BF16)
 
 
 def chunk_spec(rows, width, shift=0):
@@ -386,7 +387,7 @@
     )
     weight = gather_rows(bc_weight, "fsdp")
     spread = spread_matrix(decay_rate.shape[1], width)
-    prepared = prepare(decay_rate.T, level_codes, level_scale[None, :], count)
+    prepared = prepare(decay_rate.T, level_codes, level_scale[None, :], half)
     exps = prepared[1]
     head_bits = lax.axis_size("head").bit_length() - 1
 
@@ -402,8 +403,8 @@
     pair_b = exchange(part_b)
     hid_a, part_a = attention(*inputs, edge, positions, residual_in, weight, 0, half, count)
     pair_a = exchange(part_a)
-    state_b, gone_b = block_state(hid_b, *pair_b, exps, spread, half, count)
-    state_a, gone_a = block_state(hid_a, *pair_a, exps, spread, 0, count)
+    state_b, gone_b = block_state(hid_b, *pair_b, exps, spread, half, half)
+    state_a, gone_a = block_state(hid_a, *pair_a, exps, spread, 0, half)
     y_b = local_terms(hid_b, *pair_b, prepared, spread, state_a, half, count)
     y_a = local_terms(hid_a, *pair_a, prepared, spread, state_a, 0, count)
     state = state_a * gone_b + state_b
@@ -423,7 +424,7 @@
     carried = jnp.concatenate(carried, axis=0)
     level = row_count.bit_length()
     gain = ssm_gain[None, :]
-    ones = jnp.ones_like(gone)
+    ones = jnp.asarray(np.ones(gone.shape, np.float32))
     out = finish(level, cross, hid_a, *pair_a, prepared, spread, y_a, carried, gain, ones, None, 0, count, row_count)
     return finish(
         level, cross, hid_b, *pair_b, prepared, spread, y_b, carried, gain, gone_a, out, half, count, row_count

time: 75.1 us -> 73.8 us (0.983)
  transfers between devices with their start and end apart: 9 -> 9, of which waited for: 3 -> 4; matrix products, arithmetic and copies ran while one was open for 7% -> 6% of each run, Pallas kernels for 41% -> 41%
where the time goes in v4:
time: 73.8 us; the launch traced here: 73.4 us
  Pallas kernels  42.8 us (58%)
  starting transfers between devices  11.8 us (16%)
  waiting for transfers between devices  8.76 us (12%)
  local copies, waits for them, and re-layouts  5.78 us (8%)
  other arithmetic  4.15 us (6%)
    pallas_call x2, Pallas kernels, local_terms(): pl.pallas_call(functools.partial(local_kernel, count, inner, outer), grid...  12.1 us
    pallas_call x2, Pallas kernels, attention(): pl.pallas_call(kernel, grid=((stop - start) // count,), in_specs=specs, o...  10.8 us
    ppermute x8, starting transfers between devices, partner(): lax.ppermute(x, axis, [(i, i ^ 1 << distance) for i in range(lax.axis_siz...  9.83 us
    pallas_call x2, Pallas kernels, finish(): pl.pallas_call(functools.partial(finish_kernel, count, first_level, cross...  8.94 us
    ppermute x8, waiting for transfers between devices, partner(): lax.ppermute(x, axis, [(i, i ^ 1 << distance) for i in range(lax.axis_siz...  8.76 us
    pallas_call x2, Pallas kernels, block_state(): pl.pallas_call(functools.partial(state_kernel, count), grid=(rows // tall...  6.82 us
    pallas_call x1, Pallas kernels, prepare(): pl.pallas_call(functools.partial(prepare_kernel, count), grid=(rows // ta...  4.11 us
    unnamed x15, local copies, waits for them, and re-layouts  3.24 us
  transfers between devices with their start and end apart: 9, of which 4 were waited for; matrix products, arithmetic and copies ran while one was open for 6% of the time, Pallas kernels for 41%

profile of v4, /device:TPU:0, one launch (start us, length us, event | category | flops | bytes accessed | tf_op | source)
XLA Modules:
  0.0 73.4 jit_solution(4223582619874061174)
XLA Ops:
  0.0 0.0 copy-start.4
  0.0 0.5 collective-permute-start
  0.5 1.0 %slice.6 = bf16[128,1024]{1,0:T(8,128)(2,1)S(1)} slice(bf16[1024,1024]{1,0:T(8,128)(2,1)} %refs_2_.1), slice={[896:1024], [0:1024]} | slice | bytes 524288 | tf_op jit(solution)/shard_map/slice | solution.py:386
  1.5 1.0 %slice.7 = bf16[128,1024]{1,0:T(8,128)(2,1)S(1)} slice(bf16[1024,1024]{1,0:T(8,128)(2,1)} %refs_4_.1), slice={[896:1024], [0:1024]} | slice | bytes 524288 | tf_op jit(solution)/shard_map/slice | solution.py:386
  2.5 2.0 %collective-permute-start.2 = (bf16[256,1024]{1,0:T(8,128)(2,1)S(1)}, bf16[256,1024]{1,0:T(8,128)(2,1)S(1)}, u32[]{:S(2)}, u32[]{:S(2)}) collective-permute-start(bf16[256,1024]{1,0:T(8,128)(2,1)S(1)} %pad_maximum_fusion.2), channel_id=1, source_target_pairs={{0,1},{1,4},{4,5},{5,8},{8,9},{9,12},{12,13},{2,3},{3,6},{6,7},{7,... | collective-permute-start | bytes 1572872 | tf_op jit(solution)/shard_map/ppermute | solution.py:352
  4.5 0.0 collective-permute-done
  4.5 0.0 copy-done.4
  4.6 0.8 %pad_maximum_fusion.1.w.refs_7_ = bf16[1024,256]{1,0:T(8,128)(2,1)} fusion(bf16[512,256]{1,0:T(8,128)(2,1)S(1)} %get-tuple-element.34, bf16[512,256]{1,0:T(8,128)(2,1)S(1)} %get-tuple-element.33), kind=kLoop, calls=%fused_computation.15 | loop fusion | flops 1048576 | bytes 1048576 | tf_op jit(solution)/shard_map/concatenate | solution.py:364
  5.4 5.3 %window_attention.2 = (bf16[512,1024]{1,0:T(8,128)(2,1)}, bf16[512,256]{1,0:T(8,128)(2,1)}) custom-call(bf16[1024,1024]{1,0:T(8,128)(2,1)} %refs_0_.1, bf16[1024,1024]{1,0:T(8,128)(2,1)} %refs_2_.1, bf16[1024,1024]{1,0:T(8,128)(2,1)} %refs_2_.1, bf16[1024,1024]{1,0:T(8,128)(2,1)} %refs_4_.1, bf16[1024,1024]{1,0:T(8,128)(2,1)} %refs_4_.1, ...), custom_call_target="tpu_custom_call" | custom-call | flops 2097152000 | bytes 5242880 | tf_op jit(solution)/shard_map/window_attention/pallas_call | solution.py:158
  10.6 0.0 copy-start.5
  10.7 3.0 %collective-permute-start.1 = (bf16[512,256]{1,0:T(8,128)(2,1)}, bf16[512,256]{1,0:T(8,128)(2,1)S(1)}, u32[]{:S(2)}, u32[]{:S(2)}) collective-permute-start(bf16[512,256]{1,0:T(8,128)(2,1)} %get-tuple-element.18.p0), channel_id=1, source_target_pairs={{0,2},{2,0},{1,3},{3,1},{4,6},{6,4},{5,7},{7,5},{8,10},{10,8},{9,1... | collective-permute-start | bytes 786440 | tf_op jit(solution)/shard_map/ppermute | solution.py:356
  13.6 0.0 collective-permute-done.2.edge
  13.6 0.8 %copy-done = bf16[256,1024]{1,0:T(8,128)(2,1)} copy-done((bf16[256,1024]{1,0:T(8,128)(2,1)}, bf16[256,1024]{1,0:T(8,128)(2,1)S(1)}, u32[]{:S(2)}) %copy-start) | copy-done | bytes 524312
  14.4 5.6 %window_attention.3 = (bf16[512,1024]{1,0:T(8,128)(2,1)}, bf16[512,256]{1,0:T(8,128)(2,1)}) custom-call(bf16[256,1024]{1,0:T(8,128)(2,1)} %copy-done, bf16[1024,1024]{1,0:T(8,128)(2,1)} %refs_0_.1, bf16[1024,1024]{1,0:T(8,128)(2,1)} %refs_2_.1, bf16[1024,1024]{1,0:T(8,128)(2,1)} %refs_2_.1, bf16[1024,1024]{1,0:T(8,128)(2,1)} %refs_4_.1, ...), custom_call_target="tpu_custom_call" | custom-call | flops 2097152000 | bytes 5242880 | tf_op jit(solution)/shard_map/window_attention/pallas_call | solution.py:158
  20.0 0.1 collective-permute-start.3
  20.1 0.0 copy-done.5
  20.1 1.0 %copy.14.codes = s32[1024,18]{1,0:T(8,128)} copy(s32[1024,18]{0,1:T(8,128)S(1)} %copy-done.5) | data formatting | bytes 147456 | tf_op args[6]
  21.1 4.1 %prepare.1 = (f32[1024,16]{1,0:T(8,128)}, bf16[1024,64]{1,0:T(8,128)(2,1)}, f32[1024,18]{1,0:T(8,128)}, f32[1024,128]{1,0:T(8,128)}) custom-call(f32[16,1024]{1,0:T(8,128)} %bitcast.15, s32[1024,18]{1,0:T(8,128)} %copy.14.codes, f32[1,18]{1,0:T(1,128)} %bitcast.25), custom_call_target="tpu_custom_call" | custom-call | flops 20480000 | bytes 1572864 | tf_op jit(solution)/shard_map/prepare/pallas_call | solution.py:86
  25.2 0.0 collective-permute-done.1.p1
  25.2 0.0 copy-start.2
  25.2 0.7 copy-done.2
  25.9 3.4 %block_state.3 = (f32[128,1024]{1,0:T(8,128)}, f32[1,1024]{1,0:T(1,128)}) custom-call(bf16[512,1024]{1,0:T(8,128)(2,1)} %get-tuple-element.17.hid, bf16[512,256]{1,0:T(8,128)(2,1)} %get-tuple-element.18.p0, bf16[512,256]{1,0:T(8,128)(2,1)} %copy-done.2, bf16[1024,64]{1,0:T(8,128)(2,1)} %get-tuple-element.19.exps, bf16[32,1024]{1,0:T(8,128)(2,1)} %constant.23.clone.spread), custom_call_target="tpu_custom_call" | custom-call | flops 2097152000 | bytes 2097152 | tf_op jit(solution)/shard_map/block_state/pallas_call | solution.py:197
  29.3 0.1 collective-permute-done.3.p1
  29.4 0.7 copy-done.3
  30.1 3.4 %block_state.2 = (f32[128,1024]{1,0:T(8,128)}, f32[1,1024]{1,0:T(1,128)}) custom-call(bf16[512,1024]{1,0:T(8,128)(2,1)} %get-tuple-element.23.hid, bf16[512,256]{1,0:T(8,128)(2,1)} %get-tuple-element.24.p0, bf16[512,256]{1,0:T(8,128)(2,1)} %copy-done.3, bf16[1024,64]{1,0:T(8,128)(2,1)} %get-tuple-element.19.exps, bf16[32,1024]{1,0:T(8,128)(2,1)} %constant.23.clone.spread), custom_call_target="tpu_custom_call" | custom-call | flops 2097152000 | bytes 2097152 | tf_op jit(solution)/shard_map/block_state/pallas_call | solution.py:197
  33.6 0.0 copy-done.1
  33.6 0.0 copy-done.6
  33.6 1.1 %fusion.9 = (bf16[128,1024]{1,0:T(8,128)(2,1)S(1)}, f32[128,1024]{1,0:T(8,128)S(1)}) fusion(f32[128,1024]{1,0:T(8,128)S(1)} %copy-done.1, f32[128,1024]{1,0:T(8,128)} %get-tuple-element.25.given, f32[1024]{0:T(1024)S(1)} %bitcast.24), kind=kLoop, calls=%fused_computation.24 | loop fusion | flops 393216 | bytes 1839104 | tf_op jit(solution)/shard_map/convert_element_type | solution.py:417
  34.7 1.1 %collective-permute-start.4 = (bf16[128,1024]{1,0:T(8,128)(2,1)S(1)}, bf16[128,1024]{1,0:T(8,128)(2,1)S(1)}, u32[]{:S(2)}, u32[]{:S(2)}) collective-permute-start(bf16[128,1024]{1,0:T(8,128)(2,1)S(1)} %get-tuple-element.31), channel_id=1, source_target_pairs={{0,1},{1,0},{4,5},{5,4},{8,9},{9,8},{12,13},{13,12},{2,3},{3,2},{6... | collective-permute-start | bytes 786440 | tf_op jit(solution)/shard_map/ppermute | solution.py:356
  35.8 0.7 mul.86
  36.5 0.0 collective-permute-start.5
  36.5 1.2 %collective-permute-done.5 = f32[1,1024]{1,0:T(1,128)S(1)} collective-permute-done((f32[1,1024]{1,0:T(1,128)S(1)}, f32[1,1024]{1,0:T(1,128)S(1)}, u32[]{:S(2)}, u32[]{:S(2)}) %collective-permute-start.5) | collective-permute-done | bytes 4128 | tf_op jit(solution)/shard_map/ppermute | solution.py:356
  37.7 2.4 %collective-permute-start.7 = (f32[1,1024]{1,0:T(1,128)S(1)}, f32[1,1024]{1,0:T(1,128)S(1)}, u32[]{:S(2)}, u32[]{:S(2)}) collective-permute-start(f32[1,1024]{1,0:T(1,128)S(1)} %mul.96), channel_id=1, source_target_pairs={{0,4},{1,5},{4,0},{5,1},{8,12},{9,13},{12,8},{13,9},{2,6},{3,7},{6... | collective-permute-start | bytes 12296 | tf_op jit(solution)/shard_map/ppermute | solution.py:356
  40.1 0.0 collective-permute-done.4
  40.1 0.1 fusion.8
  40.2 0.1 collective-permute-start.6
  40.3 5.9 %local_terms.3.y = f32[512,1024]{1,0:T(8,128)} custom-call(bf16[512,1024]{1,0:T(8,128)(2,1)} %get-tuple-element.23.hid, bf16[512,256]{1,0:T(8,128)(2,1)} %get-tuple-element.24.p0, bf16[512,256]{1,0:T(8,128)(2,1)} %copy-done.3, f32[1024,16]{1,0:T(8,128)} %get-tuple-element.21.cum_ref, bf16[1024,64]{1,0:T(8,128)(2,1)} %get-tuple-element.19.exps, ...), custom_call_target="tpu_custom_call" | custom-call | flops 3145728000 | bytes 4194304 | tf_op jit(solution)/shard_map/local_terms/pallas_call | solution.py:274
  46.2 0.0 collective-permute-done.7
  46.2 2.4 %collective-permute-done.6 = bf16[128,1024]{1,0:T(8,128)(2,1)S(1)} collective-permute-done((bf16[128,1024]{1,0:T(8,128)(2,1)S(1)}, bf16[128,1024]{1,0:T(8,128)(2,1)S(1)}, u32[]{:S(2)}, u32[]{:S(2)}) %collective-permute-start.6) | collective-permute-done | bytes 262176 | tf_op jit(solution)/shard_map/ppermute | solution.py:356
  48.6 0.3 fusion
  48.9 2.7 %collective-permute-start.8 = (bf16[128,1024]{1,0:T(8,128)(2,1)S(1)}, bf16[128,1024]{1,0:T(8,128)(2,1)S(1)}, u32[]{:S(2)}, u32[]{:S(2)}) collective-permute-start(bf16[128,1024]{1,0:T(8,128)(2,1)S(1)} %get-tuple-element.36), channel_id=1, source_target_pairs={{0,8},{1,9},{4,12},{5,13},{8,0},{9,1},{12,4},{13,5},{2,10},{3,11},... | collective-permute-start | bytes 786440 | tf_op jit(solution)/shard_map/ppermute | solution.py:356
  51.5 6.2 %local_terms.2.y = f32[512,1024]{1,0:T(8,128)} custom-call(bf16[512,1024]{1,0:T(8,128)(2,1)} %get-tuple-element.17.hid, bf16[512,256]{1,0:T(8,128)(2,1)} %get-tuple-element.18.p0, bf16[512,256]{1,0:T(8,128)(2,1)} %copy-done.2, f32[1024,16]{1,0:T(8,128)} %get-tuple-element.21.cum_ref, bf16[1024,64]{1,0:T(8,128)(2,1)} %get-tuple-element.19.exps, ...), custom_call_target="tpu_custom_call" | custom-call | flops 3145728000 | bytes 4194304 | tf_op jit(solution)/shard_map/local_terms/pallas_call | solution.py:274
  57.8 5.1 %collective-permute-done.8 = bf16[128,1024]{1,0:T(8,128)(2,1)S(1)} collective-permute-done((bf16[128,1024]{1,0:T(8,128)(2,1)S(1)}, bf16[128,1024]{1,0:T(8,128)(2,1)S(1)}, u32[]{:S(2)}, u32[]{:S(2)}) %collective-permute-start.8) | collective-permute-done | bytes 262176 | tf_op jit(solution)/shard_map/ppermute | solution.py:356
  62.9 0.1 select_convert_fusion
  62.9 1.0 %pad_maximum_fusion.carried = bf16[384,1024]{1,0:T(8,128)(2,1)} fusion(bf16[128,1024]{1,0:T(8,128)(2,1)S(1)} %select_convert_fusion, bf16[128,1024]{1,0:T(8,128)(2,1)S(1)} %get-tuple-element.37, bf16[128,1024]{1,0:T(8,128)(2,1)S(1)} %get-tuple-element.35), kind=kLoop, calls=%fused_computation | loop fusion | flops 2359296 | bytes 1572864 | tf_op jit(solution)/shard_map/concatenate | solution.py:424
  63.9 0.6 broadcast_in_dim.17.begin
  64.5 4.5 %finish.2.rest_0_ = bf16[1024,1024]{1,0:T(8,128)(2,1)} custom-call(bf16[512,1024]{1,0:T(8,128)(2,1)} %get-tuple-element.23.hid, bf16[512,256]{1,0:T(8,128)(2,1)} %get-tuple-element.24.p0, bf16[512,256]{1,0:T(8,128)(2,1)} %copy-done.3, bf16[1024,64]{1,0:T(8,128)(2,1)} %get-tuple-element.19.exps, f32[1024,18]{1,0:T(8,128)} %get-tuple-element.20.lam_ref, ...), custom_call_target="tpu_custom_call" | custom-call | tf_op jit(solution)/shard_map/finish/pallas_call | solution.py:337
  69.0 4.5 %finish.3 = bf16[1024,1024]{1,0:T(8,128)(2,1)} custom-call(bf16[512,1024]{1,0:T(8,128)(2,1)} %get-tuple-element.17.hid, bf16[512,256]{1,0:T(8,128)(2,1)} %get-tuple-element.18.p0, bf16[512,256]{1,0:T(8,128)(2,1)} %copy-done.2, bf16[1024,64]{1,0:T(8,128)(2,1)} %get-tuple-element.19.exps, ...), custom_call_target="tpu_custom_call", output_to_operand_aliasing={{}: (10, {})} | custom-call | tf_op jit(solution)/shard_map/finish/pallas_call | solution.py:337
  (8 shorter events, 0.1 us)
Async XLA Ops:
  0.0 4.5 %copy-start.4 = (bf16[512,256]{1,0:T(8,128)(2,1)S(1)}, bf16[512,256]{1,0:T(8,128)(2,1)}, u32[]{:S(2)}) copy-start(bf16[512,256]{1,0:T(8,128)(2,1)} %param.16) | copy-start | bytes 786436
  0.0 4.5 %collective-permute-start = (bf16[512,256]{1,0:T(8,128)(2,1)}, bf16[512,256]{1,0:T(8,128)(2,1)S(1)}, u32[]{:S(2)}, u32[]{:S(2)}) collective-permute-start(bf16[512,256]{1,0:T(8,128)(2,1)} %param.16), channel_id=1, source_target_pairs={{0,1},{1,0},{2,3},{3,2},{4,5},{5,4},{6,7},{7,6},{8,9},{9,8},{10,11... | collective-permute-start | bytes 786440 | tf_op jit(solution)/shard_map/ppermute | solution.py:356
  2.5 11.2 %collective-permute-start.2 = (bf16[256,1024]{1,0:T(8,128)(2,1)S(1)}, bf16[256,1024]{1,0:T(8,128)(2,1)S(1)}, u32[]{:S(2)}, u32[]{:S(2)}) collective-permute-start(bf16[256,1024]{1,0:T(8,128)(2,1)S(1)} %pad_maximum_fusion.2), channel_id=1, source_target_pairs={{0,1},{1,4},{4,5},{5,8},{8,9},{9,12},{12,13},{2,3},{3,6},{6,7},{7,... | collective-permute-start | bytes 1572872 | tf_op jit(solution)/shard_map/ppermute | solution.py:352
  10.6 9.4 %copy-start.5 = (s32[1024,18]{0,1:T(8,128)S(1)}, s32[1024,18]{0,1:T(8,128)}, u32[]{:S(2)}) copy-start(s32[1024,18]{0,1:T(8,128)} %param.18) | copy-start | bytes 221188
  10.7 14.6 %collective-permute-start.1 = (bf16[512,256]{1,0:T(8,128)(2,1)}, bf16[512,256]{1,0:T(8,128)(2,1)S(1)}, u32[]{:S(2)}, u32[]{:S(2)}) collective-permute-start(bf16[512,256]{1,0:T(8,128)(2,1)} %get-tuple-element.18.p0), channel_id=1, source_target_pairs={{0,2},{2,0},{1,3},{3,1},{4,6},{6,4},{5,7},{7,5},{8,10},{10,8},{9,1... | collective-permute-start | bytes 786440 | tf_op jit(solution)/shard_map/ppermute | solution.py:356
  13.6 0.8 %copy-start = (bf16[256,1024]{1,0:T(8,128)(2,1)}, bf16[256,1024]{1,0:T(8,128)(2,1)S(1)}, u32[]{:S(2)}) copy-start(bf16[256,1024]{1,0:T(8,128)(2,1)S(1)} %collective-permute-done.2.edge) | copy-start | bytes 1572868
  20.0 9.4 %collective-permute-start.3 = (bf16[512,256]{1,0:T(8,128)(2,1)}, bf16[512,256]{1,0:T(8,128)(2,1)S(1)}, u32[]{:S(2)}, u32[]{:S(2)}) collective-permute-start(bf16[512,256]{1,0:T(8,128)(2,1)} %get-tuple-element.24.p0), channel_id=1, source_target_pairs={{0,2},{2,0},{1,3},{3,1},{4,6},{6,4},{5,7},{7,5},{8,10},{10,8},{9,1... | collective-permute-start | bytes 786440 | tf_op jit(solution)/shard_map/ppermute | solution.py:356
  25.2 0.7 copy-start.2
  29.4 0.7 copy-start.3
  30.1 3.5 %copy-start.1 = (f32[128,1024]{1,0:T(8,128)S(1)}, f32[128,1024]{1,0:T(8,128)}, u32[]{:S(2)}) copy-start(f32[128,1024]{1,0:T(8,128)} %get-tuple-element.27) | copy-start | bytes 1572868
  30.1 3.5 %copy-start.6 = (f32[1,1024]{1,0:T(1,128)S(1)}, f32[1,1024]{1,0:T(1,128)}, u32[]{:S(2)}) copy-start(f32[1,1024]{1,0:T(1,128)} %get-tuple-element.26) | copy-start | bytes 12292
  34.7 5.4 %collective-permute-start.4 = (bf16[128,1024]{1,0:T(8,128)(2,1)S(1)}, bf16[128,1024]{1,0:T(8,128)(2,1)S(1)}, u32[]{:S(2)}, u32[]{:S(2)}) collective-permute-start(bf16[128,1024]{1,0:T(8,128)(2,1)S(1)} %get-tuple-element.31), channel_id=1, source_target_pairs={{0,1},{1,0},{4,5},{5,4},{8,9},{9,8},{12,13},{13,12},{2,3},{3,2},{6... | collective-permute-start | bytes 786440 | tf_op jit(solution)/shard_map/ppermute | solution.py:356
  36.5 1.2 %collective-permute-start.5 = (f32[1,1024]{1,0:T(1,128)S(1)}, f32[1,1024]{1,0:T(1,128)S(1)}, u32[]{:S(2)}, u32[]{:S(2)}) collective-permute-start(f32[1,1024]{1,0:T(1,128)S(1)} %mul.86), channel_id=1, source_target_pairs={{0,1},{1,0},{4,5},{5,4},{8,9},{9,8},{12,13},{13,12},{2,3},{3,2},{6... | collective-permute-start | bytes 12296 | tf_op jit(solution)/shard_map/ppermute | solution.py:356
  37.7 8.5 %collective-permute-start.7 = (f32[1,1024]{1,0:T(1,128)S(1)}, f32[1,1024]{1,0:T(1,128)S(1)}, u32[]{:S(2)}, u32[]{:S(2)}) collective-permute-start(f32[1,1024]{1,0:T(1,128)S(1)} %mul.96), channel_id=1, source_target_pairs={{0,4},{1,5},{4,0},{5,1},{8,12},{9,13},{12,8},{13,9},{2,6},{3,7},{6... | collective-permute-start | bytes 12296 | tf_op jit(solution)/shard_map/ppermute | solution.py:356
  40.2 8.3 %collective-permute-start.6 = (bf16[128,1024]{1,0:T(8,128)(2,1)S(1)}, bf16[128,1024]{1,0:T(8,128)(2,1)S(1)}, u32[]{:S(2)}, u32[]{:S(2)}) collective-permute-start(bf16[128,1024]{1,0:T(8,128)(2,1)S(1)} %fusion.8), channel_id=1, source_target_pairs={{0,4},{1,5},{4,0},{5,1},{8,12},{9,13},{12,8},{13,9},{2,6},{3,7},{6... | collective-permute-start | bytes 786440 | tf_op jit(solution)/shard_map/ppermute | solution.py:356
  48.9 14.0 %collective-permute-start.8 = (bf16[128,1024]{1,0:T(8,128)(2,1)S(1)}, bf16[128,1024]{1,0:T(8,128)(2,1)S(1)}, u32[]{:S(2)}, u32[]{:S(2)}) collective-permute-start(bf16[128,1024]{1,0:T(8,128)(2,1)S(1)} %get-tuple-element.36), channel_id=1, source_target_pairs={{0,8},{1,9},{4,12},{5,13},{8,0},{9,1},{12,4},{13,5},{2,10},{3,11},... | collective-permute-start | bytes 786440 | tf_op jit(solution)/shard_map/ppermute | solution.py:356
